TPU v7x, 128 devices: a whole 4x4x4 slice. The times are simulated.
128 devices in a mesh: role: 4 (over y_lo, core), shard: 32 (over z, y_hi, x).
Axes of the slice: x: 4, y: 4 (y_hi: 2, y_lo: 2; y = y_hi * 2 + y_lo), z: 4, core: 2. Of those that a mesh axis runs over, the one named last changes fastest.
Arguments:
- gradient: bfloat16 [2560, 2560], P('shard', 'role'), may hold values from -1200 to 1200
- left_old: float32 [2560, 2560], P('shard', 'role'), may hold values from -1 to 10, as said below
- right_old: float32 [2560, 2560], P('shard', 'role'), may hold values from -1 to 10, as said below
- basis_old: bfloat16 [2560, 512], P('shard', 'role'), may hold values from -1 to 1
Outputs:
- left_stat: float32 [2560, 2560], P('shard', 'role')
- right_stat: float32 [2560, 2560], P('shard', 'role')
- left_basis: float32 [2560, 512], P('shard', 'role')
Inputs may be any that keep to these rules, and one draw needn't show every extreme that they name: `left_old`: symmetric and positive definite. `right_old`: symmetric and positive definite.
All inputs are finite; a program needn't handle non-finite values.
Results may differ from a plain program's by a relative error of at most 0.0003.
Values may be sent and summed in bfloat16 or wider, within the bound.
A program may use at most 64 MiB of HBM per device.

v0:
```python
import functools

import jax
import jax.numpy as jnp
from jax import lax
from jax.sharding import Mesh
from jax.sharding import PartitionSpec as P

SHARD = ("shard_0", "shard_1", "shard_2")
ROLE = ("role_0", "role_1")
ROLE_SHARD = ("role_0", "role_1", "shard_0", "shard_1", "shard_2")


smoothing = 0.95
clip_ratio = 4.0
epsilon_value = 1e-06


def over_pieces(x, axis):
    parts = lax.all_gather(x, axis)
    return parts.sum(axis=0)


def copy_for_each(x, axis):
    size = lax.axis_size(axis)
    return lax.all_to_all(jnp.broadcast_to(x[None], (size, *x.shape)), axis, 0, 0, tiled=True)


def joined_along(parts, dim):
    lengths = list(parts.shape[1:])
    lengths[dim] *= parts.shape[0]
    return jnp.moveaxis(parts, 0, dim).reshape(lengths)


def gathered_copies(x, axis, dim):
    parts = copy_for_each(x, axis)
    return joined_along(parts, dim)


def by_axis(x, axes):
    return functools.reduce(lax.psum, axes, x)


def all_blocks(x, axes, turns):
    parts = x
    for k in turns:
        parts = lax.all_gather(parts, axes[k])
    done = turns[::-1]
    back = [done.index(k) for k in range(len(axes))]
    parts = parts.transpose(*back, *range(len(axes), parts.ndim))
    return parts.reshape(-1, *x.shape)


def gathered_by_axis(x, axes, turns, dim):
    return joined_along(all_blocks(x, axes, turns), dim)


def taken_together(x, axis):
    everything = copy_for_each(x, axis)
    return jnp.sum(everything, axis=0)


def lower_gram(power_row, role_count, role_at):
    order_size = power_row.shape[1]
    tile_size = order_size // (2 * role_count)
    second_row = 2 * role_count - 1 - role_at

    def strip(tile_row):
        chosen = lax.dynamic_slice_in_dim(power_row, tile_row * tile_size, tile_size, 1)
        return lax.dot_general(
            chosen,
            power_row,
            (((0,), (0,)), ((), ())),
            precision=lax.Precision.HIGHEST,
            preferred_element_type=jnp.float32,
        )

    strip_first = strip(role_at)
    strip_second = strip(second_row)
    split_at = (role_at + 1) * tile_size
    packed_width = order_size + tile_size
    first_ext = jnp.concatenate(
        [strip_first, jnp.zeros((tile_size, tile_size), jnp.float32)], axis=1
    )
    padded_second = jnp.concatenate(
        [jnp.zeros((tile_size, order_size), jnp.float32), strip_second], axis=1
    )
    second_ext = lax.dynamic_slice_in_dim(padded_second, order_size - split_at, packed_width, 1)
    columns = lax.broadcasted_iota(jnp.int32, (tile_size, packed_width), 1)
    packed = jnp.where(columns < split_at, first_ext, second_ext)
    tile_sums = over_pieces(packed, SHARD)
    strips = gathered_copies(tile_sums, ROLE, 0)
    lower_part = jnp.zeros((order_size, order_size), jnp.float32)
    for member in range(role_count):
        packed_row = strips[member * tile_size : (member + 1) * tile_size]
        head = (member + 1) * tile_size
        other = 2 * role_count - 1 - member
        tail = (2 * role_count - member) * tile_size
        lower_part = lower_part.at[member * tile_size : head, :head].set(packed_row[:, :head])
        lower_part = lower_part.at[other * tile_size : (other + 1) * tile_size, :tail].set(
            packed_row[:, head : head + tail]
        )
    return jnp.tril(lower_part) + jnp.transpose(jnp.tril(lower_part, -1))


def on_device(gradient, left_old, right_old, basis_old):
    row_count, col_count = gradient.shape
    vec_count = basis_old.shape[1]
    order_size = row_count * lax.axis_size(SHARD)
    role_count = lax.axis_size(ROLE)
    role_at = lax.axis_index(ROLE)
    col_start = role_at * col_count
    vec_start = role_at * vec_count
    gradient_wide = gradient.astype(jnp.float32)
    squares = by_axis(jnp.sum(gradient_wide * gradient_wide), ROLE_SHARD)
    factor = jnp.minimum(
        1.0, clip_ratio * jnp.sqrt(jnp.float32(order_size)) / jnp.sqrt(squares + epsilon_value)
    )
    squared = factor * factor
    grad_row = gathered_copies(gradient, ROLE, 1)
    owned_cols = lax.all_to_all(grad_row, SHARD, split_axis=1, concat_axis=0, tiled=True)
    block_piece = gathered_by_axis(gradient, SHARD, (1, 0, 2), 0)
    left_term = lax.dot_general(
        gradient, block_piece, (((1,), (1,)), ((), ())), preferred_element_type=jnp.float32
    )
    right_acc = lax.dot_general(
        owned_cols, block_piece, (((0,), (0,)), ((), ())), preferred_element_type=jnp.float32
    )
    placed = lax.dynamic_update_slice_in_dim(
        jnp.zeros((row_count, order_size), jnp.float32), left_old, col_start, 1
    )
    left_row = taken_together((1.0 - smoothing) * squared * left_term + smoothing * placed, ROLE)
    left_stat = lax.dynamic_slice_in_dim(left_row, col_start, col_count, 1)
    right_stat = smoothing * right_old + (1.0 - smoothing) * squared * right_acc
    power_block = jnp.dot(
        left_row,
        gathered_copies(basis_old, SHARD, 0).astype(jnp.float32),
        precision=lax.Precision.HIGHEST,
    )
    power_row = gathered_copies(power_block, ROLE, 1)
    gram_full = lower_gram(power_row, role_count, role_at)
    factor_lower = jnp.linalg.cholesky(gram_full)
    solved = jax.scipy.linalg.solve_triangular(factor_lower, power_row.T, lower=True)
    left_basis = lax.dynamic_slice_in_dim(solved, vec_start, vec_count, 0).T
    return (left_stat, right_stat, left_basis)


def solution(mesh):
    finer = Mesh(
        mesh.devices.reshape(2, 2, 4, 2, 4), ("role_0", "role_1", "shard_0", "shard_1", "shard_2")
    )
    return jax.shard_map(
        on_device,
        mesh=finer,
        in_specs=(P(SHARD, ROLE), P(SHARD, ROLE), P(SHARD, ROLE), P(SHARD, ROLE)),
        out_specs=(P(SHARD, ROLE), P(SHARD, ROLE), P(SHARD, ROLE)),
        check_vma=False,
    )
```

profile of v0, /device:TPU:1, one launch (start us, length us, event | category | flops | bytes accessed | tf_op | source)
XLA Modules:
  0.0 409.6 jit_solution(4335116973042606115)
XLA Ops:
  7.2 7.0 %all-gather = bf16[160,640]{1,0:T(8,128)(2,1)S(1)} all-gather(bf16[80,640]{1,0:T(8,128)(2,1)} %param.20), channel_id=2, replica_groups=mesh['role_0'=2,'role_1'=2,'shard_0'=4,'shard_1'=2,'shard_2'=4] {'shard_1'}, dimensions={0}, use_global_device_ids=true | all-gather | bytes 307200 | tf_op jit(solution)/shard_map/all_gather | solution.py:47
  14.3 13.4 %all-gather.1 = bf16[8,80,640]{2,1,0:T(8,128)(2,1)} all-gather(bf16[2,80,640]{2,1,0:T(8,128)(2,1)S(1)} %bitcast.96), channel_id=3, replica_groups=mesh['role_0'=2,'role_1'=2,'shard_0'=4,'shard_1'=2,'shard_2'=4] {'shard_0'}, dimensions={0}, use_global_device_ids=true | all-gather | bytes 1024000 | tf_op jit(solution)/shard_map/all_gather | solution.py:47
  27.7 1.6 multiply_reduce_fusion
  29.3 4.4 %psum.35 = f32[]{:T(128)} all-reduce(f32[]{:T(128)} %multiply_reduce_fusion), channel_id=1, replica_groups=mesh['role_0'=2,'role_1'=2,'shard_0'=4,'shard_1'=2,'shard_2'=4] {'role_0'}, use_global_device_ids=true, to_apply=%region_1.0 | all-reduce | flops 1 | bytes 8 | tf_op jit(solution)/shard_map/psum | solution.py:41
  33.7 7.4 %psum.36 = f32[]{:T(128)} all-reduce(f32[]{:T(128)} %psum.35), channel_id=1, replica_groups=mesh['role_0'=2,'role_1'=2,'shard_0'=4,'shard_1'=2,'shard_2'=4] {'role_1'}, use_global_device_ids=true, to_apply=%region_2.0 | all-reduce | flops 1 | bytes 8 | tf_op jit(solution)/shard_map/psum | solution.py:41
  41.1 9.9 %psum.37 = f32[]{:T(128)} all-reduce(f32[]{:T(128)} %psum.36), channel_id=1, replica_groups=mesh['role_0'=2,'role_1'=2,'shard_0'=4,'shard_1'=2,'shard_2'=4] {'shard_0'}, use_global_device_ids=true, to_apply=%region_3.0 | all-reduce | flops 1 | bytes 8 | tf_op jit(solution)/shard_map/psum | solution.py:41
  51.0 6.2 %psum.38 = f32[]{:T(128)} all-reduce(f32[]{:T(128)} %psum.37), channel_id=1, replica_groups=mesh['role_0'=2,'role_1'=2,'shard_0'=4,'shard_1'=2,'shard_2'=4] {'shard_1'}, use_global_device_ids=true, to_apply=%region_4.0 | all-reduce | flops 1 | bytes 8 | tf_op jit(solution)/shard_map/psum | solution.py:41
  57.2 10.1 %psum.39 = f32[]{:T(128)} all-reduce(f32[]{:T(128)} %psum.38), channel_id=1, replica_groups=mesh['role_0'=2,'role_1'=2,'shard_0'=4,'shard_1'=2,'shard_2'=4] {'shard_2'}, use_global_device_ids=true, to_apply=%region_5.0 | all-reduce | flops 1 | bytes 8 | tf_op jit(solution)/shard_map/psum | solution.py:41
  68.0 1.0 broadcast_in_dim.17
  69.0 1.6 constant_dynamic-update-slice_fusion.1
  70.6 2.4 all-gather.7.cloned.1.call-done
  73.0 2.3 copy.23
  75.3 2.3 fusion
  78.0 42.2 %all_to_all.44 = f32[4,80,2560]{2,1,0:T(8,128)} all-to-all(f32[4,80,2560]{2,1,0:T(8,128)S(1)} %broadcast_in_dim.18), channel_id=1, replica_groups=mesh['role_0'=2,'role_1'=2,'shard_0'=4,'shard_1'=2,'shard_2'=4] {'role_0..., dimensions={0} | all-to-all | bytes 6553600 | tf_op jit(solution)/shard_map/all_to_all | solution.py:26
  120.2 0.9 broadcast_in_dim.20
  121.1 7.5 %all-to-all-start.3 = ((bf16[32,80,128]{2,1,0:T(8,128)(2,1)}), bf16[32,80,128]{2,1,0:T(8,128)(2,1)}, u32[]{:S(2)}, u32[]{:S(2)}) async-start(bf16[32,80,128]{2,1,0:T(8,128)(2,1)} %broadcast_in_dim.20), calls=%async_computation.3 | async-start | bytes 1310720 | tf_op jit(solution)/shard_map/all_to_all | solution.py:26
  128.6 3.1 reduce_sum.28
  131.7 9.2 %all-to-all-done.3 = bf16[32,80,128]{2,1,0:T(8,128)(2,1)} async-done(((bf16[32,80,128]{2,1,0:T(8,128)(2,1)}), bf16[32,80,128]{2,1,0:T(8,128)(2,1)}, u32[]{:S(2)}, u32[]{:S(2)}) %all-to-all-start.3) | async-done | bytes 655392 | tf_op jit(solution)/shard_map/all_to_all | solution.py:26
  140.9 1.8 fusion.46
  142.8 0.7 broadcast_in_dim.21
  143.5 6.2 %all-to-all-start.4 = ((f32[4,80,128]{2,1,0:T(8,128)}), f32[4,80,128]{2,1,0:T(8,128)S(1)}, u32[]{:S(2)}, u32[]{:S(2)}) async-start(f32[4,80,128]{2,1,0:T(8,128)} %broadcast_in_dim.21), calls=%async_computation.4 | async-start | bytes 327680 | tf_op jit(solution)/shard_map/all_to_all | solution.py:26
  149.7 3.9 all-to-all-done.4
  153.5 0.7 fusion.44
  154.2 0.4 fusion.38
  154.6 0.4 fusion.36
  155.0 0.8 fusion.9
  155.9 11.8 %all_to_all.45 = bf16[4,80,640]{2,1,0:T(8,128)(2,1)S(1)} all-to-all(bf16[4,80,640]{2,1,0:T(8,128)(2,1)S(1)} %broadcast_in_dim.19), channel_id=1, replica_groups=mesh['role_0'=2,'role_1'=2,'shard_0'=4,'shard_1'=2,'shard_2'=4] {'role_0..., dimensions={0} | all-to-all | bytes 819200 | tf_op jit(solution)/shard_map/all_to_all | solution.py:26
  167.7 0.9 copy.24
  168.6 2.6 all_to_all.31
  171.2 2.2 copy.25
  173.4 4.6 %all-to-all-start.2 = ((bf16[80,32,80]{2,0,1:T(8,128)(2,1)}), bf16[80,32,80]{2,0,1:T(8,128)(2,1)}, u32[]{:S(2)}, u32[]{:S(2)}) async-start(bf16[80,32,80]{2,0,1:T(8,128)(2,1)} %copy.25), calls=%async_computation.2 | async-start | bytes 1310720 | tf_op jit(solution)/shard_map/all_to_all | solution.py:121
  178.1 61.2 %all-gather.9.cloned.1.call-done = f32[2048,576]{1,0:T(8,128)} async-done(((f32[64,576]{1,0:T(8,128)}), f32[2048,576]{1,0:T(8,128)}) %all-gather.9.cloned.1.call-update) | async-done | bytes 4718608 | tf_op jit(solution)/shard_map/all_gather | solution.py:20
  239.3 2.8 reduce_sum.29
  242.1 0.9 broadcast_in_dim.22
  243.0 5.2 %all-to-all-start.5 = ((f32[4,64,576]{2,1,0:T(8,128)}), f32[4,64,576]{2,1,0:T(8,128)}, u32[]{:S(2)}, u32[]{:S(2)}) async-start(f32[4,64,576]{2,1,0:T(8,128)} %broadcast_in_dim.22), calls=%async_computation.5 | async-start | bytes 1310720 | tf_op jit(solution)/shard_map/all_to_all | solution.py:26
  248.2 2.5 fusion.1
  250.7 1.6 constant_dynamic-slice_fusion.1
  252.3 5.4 %all-to-all-done.5 = f32[4,64,576]{2,1,0:T(8,128)} async-done(((f32[4,64,576]{2,1,0:T(8,128)}), f32[4,64,576]{2,1,0:T(8,128)}, u32[]{:S(2)}, u32[]{:S(2)}) %all-to-all-start.5) | async-done | bytes 589856 | tf_op jit(solution)/shard_map/all_to_all | solution.py:26
  257.7 1.2 slice_bitcast_fusion
  259.2 1.7 scatter.31
  260.8 1.6 scatter.34
  262.5 1.9 scatter.39
  265.6 11.7 %cholesky.103 = f32[128,128]{1,0:T(8,128)S(1)} custom-call(f32[128,128]{1,0:T(8,128)S(1)} %cholesky.263), custom_call_target="Cholesky" | custom-call | tf_op jit(solution)/shard_map/jit(cholesky)/cholesky | solution.py:142
  277.5 9.8 %custom-call.31 = f32[1,128,128]{1,2,0:T(8,128)S(1)} custom-call(f32[1,128,128]{2,1,0:T(8,128)S(1)} %get-tuple-element.132), custom_call_target="InvertDiagBlocksLowerTriangular" | custom-call | tf_op jit(solution)/shard_map/jit(cholesky)/cholesky | solution.py:142
  288.0 11.7 %cholesky.215 = f32[128,128]{1,0:T(8,128)S(1)} custom-call(f32[128,128]{1,0:T(8,128)S(1)} %cholesky.267), custom_call_target="Cholesky" | custom-call | tf_op jit(solution)/shard_map/jit(cholesky)/cholesky | solution.py:142
  299.8 10.0 %custom-call.32 = f32[1,128,128]{1,2,0:T(8,128)S(1)} custom-call(f32[1,128,128]{2,1,0:T(8,128)S(1)} %get-tuple-element.129), custom_call_target="InvertDiagBlocksLowerTriangular" | custom-call | tf_op jit(solution)/shard_map/jit(cholesky)/cholesky | solution.py:142
  310.4 11.7 %cholesky.236 = f32[128,128]{1,0:T(8,128)S(1)} custom-call(f32[128,128]{1,0:T(8,128)S(1)} %cholesky.272), custom_call_target="Cholesky" | custom-call | tf_op jit(solution)/shard_map/jit(cholesky)/cholesky | solution.py:142
  322.2 0.7 compare_reduce_fusion.1
  322.9 9.8 %custom-call.33 = f32[1,128,128]{1,2,0:T(8,128)S(1)} custom-call(f32[1,128,128]{2,1,0:T(8,128)S(1)} %get-tuple-element.126), custom_call_target="InvertDiagBlocksLowerTriangular" | custom-call | tf_op jit(solution)/shard_map/jit(cholesky)/cholesky | solution.py:142
  333.3 11.9 %cholesky.253 = f32[128,128]{1,0:T(8,128)S(1)} custom-call(f32[128,128]{1,0:T(8,128)S(1)} %convolution_subtract_fusion.2), custom_call_target="Cholesky" | custom-call | tf_op jit(solution)/shard_map/jit(cholesky)/cholesky | solution.py:142
  345.3 0.6 compare_reduce_fusion
  345.9 0.7 compare_reduce_fusion.2
  349.3 10.6 %while.9 = (s32[]{:T(128)}, f32[512,512]{1,0:T(8,128)S(1)}, s32[4,2]{0,1:T(2,128)S(1)}, f32[4,128,128]{2,1,0:T(8,128)}, s32[]{:T(128)}) while((s32[]{:T(128)}, f32[512,512]{1,0:T(8,128)S(1)}, s32[4,2]{0,1:T(2,128)S(1)}, f32[4,128,128]{2,1,0:T(8,128)}, s32[]{:T(128)}) %tuple.67), condition=%wide.while_cond.8, body=%wide.while_body.8.sunk | while | flops 2 | bytes 132205 | solution.py:143
  349.4 0.6 fusion.62
  350.0 2.0 bitcast_dynamic-update-slice_fusion.2
  352.0 0.6 fusion.62
  352.6 2.0 bitcast_dynamic-update-slice_fusion.2
  354.6 0.6 fusion.62
  355.2 2.0 bitcast_dynamic-update-slice_fusion.2
  357.3 0.6 fusion.62
  357.9 2.0 bitcast_dynamic-update-slice_fusion.2
  359.8 40.1 %custom-call.34 = f32[4,128,128]{1,2,0:T(8,128)S(1)} custom-call(f32[4,128,128]{2,1,0:T(8,128)} %get-tuple-element.106), custom_call_target="InvertDiagBlocksLowerTriangular" | custom-call | tf_op jit(solution)/shard_map/jit(_solve_triangular)/triangular_solve | solution.py:143
  401.1 0.4 convolution_subtract_fusion.3
  401.7 0.6 fusion.34
  (57 shorter events, 5.9 us)
Async XLA Ops:
  7.2 65.8 %all-gather.7.cloned.1.call-start = ((), (), s32[]{:S(2)}) async-start(), calls=%async_computation.6 | async-start | bytes 4096000 | tf_op jit(solution)/shard_map/all_gather | solution.py:47
  73.0 2.3 copy-start
  78.0 42.2 %copy-start.2 = (bf16[80,128]{1,0:T(8,128)(2,1)S(1)}, bf16[80,128]{1,0:T(8,128)(2,1)}, u32[]{:S(2)}) copy-start(bf16[80,128]{1,0:T(8,128)(2,1)} %param.23) | copy-start | bytes 61444
  121.1 19.8 %all-to-all-start.3 = ((bf16[32,80,128]{2,1,0:T(8,128)(2,1)}), bf16[32,80,128]{2,1,0:T(8,128)(2,1)}, u32[]{:S(2)}, u32[]{:S(2)}) async-start(bf16[32,80,128]{2,1,0:T(8,128)(2,1)} %broadcast_in_dim.20), calls=%async_computation.3 | async-start | bytes 1310720 | tf_op jit(solution)/shard_map/all_to_all | solution.py:26
  143.5 10.1 %all-to-all-start.4 = ((f32[4,80,128]{2,1,0:T(8,128)}), f32[4,80,128]{2,1,0:T(8,128)S(1)}, u32[]{:S(2)}, u32[]{:S(2)}) async-start(f32[4,80,128]{2,1,0:T(8,128)} %broadcast_in_dim.21), calls=%async_computation.4 | async-start | bytes 327680 | tf_op jit(solution)/shard_map/all_to_all | solution.py:26
  149.7 89.6 %all-gather.9.cloned.1.call-start = ((), (), s32[]{:S(2)}) async-start(), calls=%async_computation.7 | async-start | bytes 5406720 | tf_op jit(solution)/shard_map/all_gather | solution.py:20
  173.4 68.7 %all-to-all-start.2 = ((bf16[80,32,80]{2,0,1:T(8,128)(2,1)}), bf16[80,32,80]{2,0,1:T(8,128)(2,1)}, u32[]{:S(2)}, u32[]{:S(2)}) async-start(bf16[80,32,80]{2,0,1:T(8,128)(2,1)} %copy.25), calls=%async_computation.2 | async-start | bytes 1310720 | tf_op jit(solution)/shard_map/all_to_all | solution.py:121
  243.0 14.7 %all-to-all-start.5 = ((f32[4,64,576]{2,1,0:T(8,128)}), f32[4,64,576]{2,1,0:T(8,128)}, u32[]{:S(2)}, u32[]{:S(2)}) async-start(f32[4,64,576]{2,1,0:T(8,128)} %broadcast_in_dim.22), calls=%async_computation.5 | async-start | bytes 1310720 | tf_op jit(solution)/shard_map/all_to_all | solution.py:26
  287.3 112.6 %copy-start.1 = (f32[512,80]{0,1:T(8,128)S(1)}, f32[512,80]{0,1:T(8,128)}, u32[]{:S(2)}) copy-start(f32[512,80]{0,1:T(8,128)} %get-tuple-element.121) | copy-start | bytes 491524
Sparse Core Ops, SparseCore 0:
  27.8 45.1 all-gather.6
  156.0 83.2 all-gather.8
where the time goes:
time: 417 us; the launch traced here: 410 us
  other arithmetic  129 us (31%)
  blocking collectives  113 us (27%)
  waiting for transfers between devices  82.1 us (20%)
  local copies, waits for them, and re-layouts  33.8 us (8%)
  starting transfers between devices  23.6 us (6%)
  between operations  18.1 us (4%)
  matrix products  10.9 us (3%)
    another operation x14, other arithmetic, on_device(): factor_lower = jnp.linalg.cholesky(gram_full)  78.9 us
    all_gather x1, waiting for transfers between devices, over_pieces(): parts = lax.all_gather(x, axis)  61.2 us
    all_to_all x2, blocking collectives, copy_for_each(): lax.all_to_all(jnp.broadcast_to(x[None], (size, *x.shape)), axis, 0, 0, t...  54 us
    another operation x3, other arithmetic, on_device(): jax.scipy.linalg.solve_triangular(factor_lower, power_row.T, lower=True)  40.3 us
    psum x5, blocking collectives, by_axis(): return functools.reduce(lax.psum, axes, x)  38 us
    all_gather x2, blocking collectives, all_blocks(): parts = lax.all_gather(parts, axes[k])  20.5 us
    all_to_all x3, starting transfers between devices, copy_for_each(): lax.all_to_all(jnp.broadcast_to(x[None], (size, *x.shape)), axis, 0, 0, t...  18.9 us
    all_to_all x3, waiting for transfers between devices, copy_for_each(): lax.all_to_all(jnp.broadcast_to(x[None], (size, *x.shape)), axis, 0, 0, t...  18.4 us
  transfers between devices with their start and end apart: 6, of which 5 were waited for; matrix products, arithmetic and copies ran while one was open for 4% of the time, Pallas kernels for 0%

commit v1 on v0

--- a/solution.py
+++ b/solution.py
@@ -3,6 +3,8 @@
 import jax
 import jax.numpy as jnp
 from jax import lax
+from jax.experimental import pallas as pl
+from jax.experimental.pallas import tpu as pltpu
 from jax.sharding import Mesh
 from jax.sharding import PartitionSpec as P
 
@@ -14,6 +16,66 @@
 smoothing = 0.95
 clip_ratio = 4.0
 epsilon_value = 1e-06
+
+
+HI = lax.Precision.HIGHEST
+TN = (((0,), (0,)), ((), ()))
+NT = (((1,), (1,)), ((), ()))
+
+def dot(a, b, dims):
+    return lax.dot_general(a, b, dims, precision=HI, preferred_element_type=jnp.float32)
+
+def eliminate(d_ref):
+    n = d_ref.shape[0]
+    sub = lax.broadcasted_iota(jnp.int32, (8, n), 0)
+    lane = lax.broadcasted_iota(jnp.int32, (8, n), 1)
+    for at in range(0, n, 8):
+        rows = d_ref[at:at + 8, :]
+        cols = [jnp.broadcast_to(rows[:, at + j:at + j + 1], (8, n)) for j in range(8)]
+        rows = jnp.where((lane >= at) & (lane < at + 8), (lane - at == sub).astype(jnp.float32), rows)
+        for j in range(8):
+            scale = lax.rsqrt(jnp.broadcast_to(cols[j][j:j + 1, :], (8, n)))
+            below = jnp.where(sub > j, cols[j] * scale, 0.0)
+            pivot = jnp.broadcast_to(rows[j:j + 1, :], (8, n)) * scale
+            rows = jnp.where(sub == j, pivot, rows - below * pivot)
+            for k in range(j + 1, 8):
+                cols[k] = cols[k] - below * (jnp.broadcast_to(cols[k][j:j + 1, :], (8, n)) * scale)
+        d_ref[at:at + 8, :] = rows
+        if at + 8 < n:
+            change = dot(rows, rows, TN)
+            rest = d_ref[at + 8:, :]
+            lanes = lax.broadcasted_iota(jnp.int32, rest.shape, 1)
+            rest = jnp.where((lanes >= at) & (lanes < at + 8), 0.0, rest)
+            d_ref[at + 8:, :] = rest - change[at + 8:, :]
+
+def factor_kernel(gram_ref, w_ref, q_ref, m_ref, d_ref):
+    order = gram_ref.shape[0]
+    total = order + w_ref.shape[0]
+    n = 128
+    m_ref[:order, :] = gram_ref[...]
+    m_ref[order:, :] = w_ref[...]
+    row = lax.broadcasted_iota(jnp.int32, (n, n), 0)
+    col = lax.broadcasted_iota(jnp.int32, (n, n), 1)
+    for at in range(0, order, n):
+        end = at + n
+        d_ref[...] = m_ref[at:end, at:end]
+        eliminate(d_ref)
+        inverse = jnp.where(col <= row, d_ref[...], 0.0)
+        panel = dot(m_ref[end:, at:end], inverse, NT)
+        q_ref[:, at:end] = panel[order - end:, :]
+        if end < order:
+            m_ref[end:, end:] = m_ref[end:, end:] - dot(panel, panel[:order - end, :], NT)
+
+def chol_q(gram, w):
+    order, rows = gram.shape[0], w.shape[0]
+    return pl.pallas_call(
+        factor_kernel,
+        out_shape=jax.ShapeDtypeStruct((rows, order), jnp.float32),
+        in_specs=[pl.BlockSpec(memory_space=pltpu.VMEM)] * 2,
+        out_specs=pl.BlockSpec(memory_space=pltpu.VMEM),
+        scratch_shapes=[pltpu.VMEM((order + rows, order), jnp.float32), pltpu.VMEM((128, 128), jnp.float32)],
+        compiler_params=pltpu.CompilerParams(vmem_limit_bytes=32 << 20),
+    )(gram, w)
 
 
 def over_pieces(x, axis):
@@ -139,9 +201,8 @@
     )
     power_row = gathered_copies(power_block, ROLE, 1)
     gram_full = lower_gram(power_row, role_count, role_at)
-    factor_lower = jnp.linalg.cholesky(gram_full)
-    solved = jax.scipy.linalg.solve_triangular(factor_lower, power_row.T, lower=True)
-    left_basis = lax.dynamic_slice_in_dim(solved, vec_start, vec_count, 0).T
+    solved = chol_q(gram_full, power_row)
+    left_basis = lax.dynamic_slice_in_dim(solved, vec_start, vec_count, 1)
     return (left_stat, right_stat, left_basis)
 
 

time: 417 us -> 322 us (0.77); the launches traced: 410 us -> 321 us
  other arithmetic: 129 us -> 9.28 us
  Pallas kernels: 0 us -> 32.5 us
    another operation x17 -> x0, other arithmetic: 119 us -> none  [the longest x14 78.9 us: on_device(): factor_lower = jnp.linalg.cholesky(gram_full)]
    pallas_call x0 -> x1, Pallas kernels: none -> 32.5 us  [chol_q(): pl.pallas_call(factor_kernel, out_shape=jax.ShapeDtypeStruct((rows, order...]
    another operation x17 -> x0, local copies, waits for them, and re-layouts: 10.7 us -> none
    scatter x4, local copies, waits for them, and re-layouts: 3.68 us -> 10.4 us  [lower_gram(): lower_part.at[other * tile_size:(other + 1) * tile_size, :tail]]
    scatter x4, local copies, waits for them, and re-layouts: 1.74 us -> 7.6 us  [lower_gram(): lower_part.at[member * tile_size:head, :head].set(packed_row[:, :head])]
  transfers between devices with their start and end apart: 6 -> 6, of which waited for: 5 -> 5; matrix products, arithmetic and copies ran while one was open for 4% -> 6% of each run, Pallas kernels for 0% -> 0%
where the time goes in v1:
time: 322 us; the launch traced here: 321 us
  blocking collectives  113 us (35%)
  waiting for transfers between devices  82.2 us (26%)
  local copies, waits for them, and re-layouts  37.9 us (12%)
  Pallas kernels  32.5 us (10%)
  starting transfers between devices  24.2 us (8%)
  between operations  15 us (5%)
  other arithmetic  9.28 us (3%)
  matrix products  7.38 us (2%)
    all_gather x1, waiting for transfers between devices, over_pieces(): parts = lax.all_gather(x, axis)  61.3 us
    all_to_all x2, blocking collectives, copy_for_each(): lax.all_to_all(jnp.broadcast_to(x[None], (size, *x.shape)), axis, 0, 0, t...  54 us
    psum x5, blocking collectives, by_axis(): return functools.reduce(lax.psum, axes, x)  38 us
    pallas_call x1, Pallas kernels, chol_q(): pl.pallas_call(factor_kernel, out_shape=jax.ShapeDtypeStruct((rows, order...  32.5 us
    all_gather x2, blocking collectives, all_blocks(): parts = lax.all_gather(parts, axes[k])  20.5 us
    all_to_all x3, starting transfers between devices, copy_for_each(): lax.all_to_all(jnp.broadcast_to(x[None], (size, *x.shape)), axis, 0, 0, t...  19.5 us
    all_to_all x3, waiting for transfers between devices, copy_for_each(): lax.all_to_all(jnp.broadcast_to(x[None], (size, *x.shape)), axis, 0, 0, t...  18.5 us
    scatter x4, local copies, waits for them, and re-layouts, lower_gram(): lower_part.at[other * tile_size:(other + 1) * tile_size, :tail]  10.4 us
  transfers between devices with their start and end apart: 6, of which 5 were waited for; matrix products, arithmetic and copies ran while one was open for 6% of the time, Pallas kernels for 0%

profile of v1, /device:TPU:1, one launch (start us, length us, event | category | flops | bytes accessed | tf_op | source)
XLA Modules:
  0.0 321.0 jit_solution(5192074120744516704)
XLA Ops:
  7.2 0.0 all-gather.7.cloned.1.call-start
  7.2 7.0 %all-gather = bf16[160,640]{1,0:T(8,128)(2,1)S(1)} all-gather(bf16[80,640]{1,0:T(8,128)(2,1)} %param.20), channel_id=2, replica_groups=mesh['role_0'=2,'role_1'=2,'shard_0'=4,'shard_1'=2,'shard_2'=4] {'shard_1'}, dimensions={0}, use_global_device_ids=true | all-gather | bytes 307200 | tf_op jit(solution)/shard_map/all_gather | solution.py:109
  14.3 13.4 %all-gather.1 = bf16[8,80,640]{2,1,0:T(8,128)(2,1)} all-gather(bf16[2,80,640]{2,1,0:T(8,128)(2,1)S(1)} %bitcast.46), channel_id=3, replica_groups=mesh['role_0'=2,'role_1'=2,'shard_0'=4,'shard_1'=2,'shard_2'=4] {'shard_0'}, dimensions={0}, use_global_device_ids=true | all-gather | bytes 1024000 | tf_op jit(solution)/shard_map/all_gather | solution.py:109
  27.7 0.0 all-gather.7.cloned.1.call-update
  27.7 1.6 multiply_reduce_fusion
  29.3 4.4 %psum.35 = f32[]{:T(128)} all-reduce(f32[]{:T(128)} %multiply_reduce_fusion), channel_id=1, replica_groups=mesh['role_0'=2,'role_1'=2,'shard_0'=4,'shard_1'=2,'shard_2'=4] {'role_0'}, use_global_device_ids=true, to_apply=%region_1.0 | all-reduce | flops 1 | bytes 8 | tf_op jit(solution)/shard_map/psum | solution.py:103
  33.7 7.4 %psum.36 = f32[]{:T(128)} all-reduce(f32[]{:T(128)} %psum.35), channel_id=1, replica_groups=mesh['role_0'=2,'role_1'=2,'shard_0'=4,'shard_1'=2,'shard_2'=4] {'role_1'}, use_global_device_ids=true, to_apply=%region_2.0 | all-reduce | flops 1 | bytes 8 | tf_op jit(solution)/shard_map/psum | solution.py:103
  41.1 9.9 %psum.37 = f32[]{:T(128)} all-reduce(f32[]{:T(128)} %psum.36), channel_id=1, replica_groups=mesh['role_0'=2,'role_1'=2,'shard_0'=4,'shard_1'=2,'shard_2'=4] {'shard_0'}, use_global_device_ids=true, to_apply=%region_3.0 | all-reduce | flops 1 | bytes 8 | tf_op jit(solution)/shard_map/psum | solution.py:103
  51.0 6.2 %psum.38 = f32[]{:T(128)} all-reduce(f32[]{:T(128)} %psum.37), channel_id=1, replica_groups=mesh['role_0'=2,'role_1'=2,'shard_0'=4,'shard_1'=2,'shard_2'=4] {'shard_1'}, use_global_device_ids=true, to_apply=%region_4.0 | all-reduce | flops 1 | bytes 8 | tf_op jit(solution)/shard_map/psum | solution.py:103
  57.2 10.1 %psum.39 = f32[]{:T(128)} all-reduce(f32[]{:T(128)} %psum.38), channel_id=1, replica_groups=mesh['role_0'=2,'role_1'=2,'shard_0'=4,'shard_1'=2,'shard_2'=4] {'shard_2'}, use_global_device_ids=true, to_apply=%region_5.0 | all-reduce | flops 1 | bytes 8 | tf_op jit(solution)/shard_map/psum | solution.py:103
  68.0 1.0 broadcast_in_dim.16
  69.0 1.6 constant_dynamic-update-slice_fusion
  70.6 2.4 all-gather.7.cloned.1.call-done
  73.0 2.3 copy.23
  75.3 0.0 copy-done
  75.3 2.3 fusion
  77.6 0.4 broadcast_in_dim.17
  78.0 0.0 copy-start.1
  78.0 42.2 %all_to_all.44 = f32[4,80,2560]{2,1,0:T(8,128)} all-to-all(f32[4,80,2560]{2,1,0:T(8,128)S(1)} %broadcast_in_dim.17), channel_id=1, replica_groups=mesh['role_0'=2,'role_1'=2,'shard_0'=4,'shard_1'=2,'shard_2'=4] {'role_0..., dimensions={0} | all-to-all | bytes 6553600 | tf_op jit(solution)/shard_map/all_to_all | solution.py:88
  120.2 0.9 broadcast_in_dim.19
  121.1 7.5 %all-to-all-start.3 = ((bf16[32,80,128]{2,1,0:T(8,128)(2,1)}), bf16[32,80,128]{2,1,0:T(8,128)(2,1)}, u32[]{:S(2)}, u32[]{:S(2)}) async-start(bf16[32,80,128]{2,1,0:T(8,128)(2,1)} %broadcast_in_dim.19), calls=%async_computation.3 | async-start | bytes 1310720 | tf_op jit(solution)/shard_map/all_to_all | solution.py:88
  128.6 3.1 reduce_sum.28
  131.7 9.2 %all-to-all-done.3 = bf16[32,80,128]{2,1,0:T(8,128)(2,1)} async-done(((bf16[32,80,128]{2,1,0:T(8,128)(2,1)}), bf16[32,80,128]{2,1,0:T(8,128)(2,1)}, u32[]{:S(2)}, u32[]{:S(2)}) %all-to-all-start.3) | async-done | bytes 655392 | tf_op jit(solution)/shard_map/all_to_all | solution.py:88
  140.9 1.8 fusion.11
  142.8 0.7 broadcast_in_dim.20
  143.5 6.8 %all-to-all-start.4 = ((f32[4,80,128]{2,1,0:T(8,128)}), f32[4,80,128]{2,1,0:T(8,128)}, u32[]{:S(2)}, u32[]{:S(2)}) async-start(f32[4,80,128]{2,1,0:T(8,128)} %broadcast_in_dim.20), calls=%async_computation.4 | async-start | bytes 327680 | tf_op jit(solution)/shard_map/all_to_all | solution.py:88
  150.3 0.0 all-gather.9.cloned.1.call-start
  150.3 4.0 %all-to-all-done.4 = f32[4,80,128]{2,1,0:T(8,128)} async-done(((f32[4,80,128]{2,1,0:T(8,128)}), f32[4,80,128]{2,1,0:T(8,128)}, u32[]{:S(2)}, u32[]{:S(2)}) %all-to-all-start.4) | async-done | bytes 163872 | tf_op jit(solution)/shard_map/all_to_all | solution.py:88
  154.3 0.9 copy_bitcast_fusion.w_ref
  155.2 0.4 fusion.6
  155.6 0.4 fusion.4
  156.0 0.8 fusion.3
  156.8 0.0 all-gather.9.cloned.1.call-update
  156.9 11.8 %all_to_all.45 = bf16[4,80,640]{2,1,0:T(8,128)(2,1)S(1)} all-to-all(bf16[4,80,640]{2,1,0:T(8,128)(2,1)S(1)} %broadcast_in_dim.18), channel_id=1, replica_groups=mesh['role_0'=2,'role_1'=2,'shard_0'=4,'shard_1'=2,'shard_2'=4] {'role_0..., dimensions={0} | all-to-all | bytes 819200 | tf_op jit(solution)/shard_map/all_to_all | solution.py:88
  168.7 0.9 copy.24
  169.6 2.6 all_to_all.31
  172.2 2.2 copy.25
  174.4 4.6 %all-to-all-start.2 = ((bf16[80,32,80]{2,0,1:T(8,128)(2,1)}), bf16[80,32,80]{2,0,1:T(8,128)(2,1)}, u32[]{:S(2)}, u32[]{:S(2)}) async-start(bf16[80,32,80]{2,0,1:T(8,128)(2,1)} %copy.25), calls=%async_computation.2 | async-start | bytes 1310720 | tf_op jit(solution)/shard_map/all_to_all | solution.py:183
  179.0 61.3 %all-gather.9.cloned.1.call-done = f32[2048,576]{1,0:T(8,128)} async-done(((f32[64,576]{1,0:T(8,128)}), f32[2048,576]{1,0:T(8,128)}) %all-gather.9.cloned.1.call-update) | async-done | bytes 4718608 | tf_op jit(solution)/shard_map/all_gather | solution.py:82
  240.3 3.4 %reduce_sum.29 = f32[64,576]{1,0:T(8,128)} reduce(f32[32,64,576]{2,1,0:T(8,128)} %bitcast.34, f32[]{:T(128)} %constant.251.clone.1), dimensions={0}, to_apply=%region_7.8 | reduce | flops 1142784 | bytes 4866052 | tf_op jit(solution)/shard_map/reduce_sum | solution.py:83
  243.7 0.0 all-to-all-done.2
  243.7 1.8 broadcast_in_dim.21
  245.5 5.2 %all-to-all-start.5 = ((f32[4,64,576]{2,1,0:T(8,128)}), f32[4,64,576]{2,1,0:T(8,128)}, u32[]{:S(2)}, u32[]{:S(2)}) async-start(f32[4,64,576]{2,1,0:T(8,128)} %broadcast_in_dim.21), calls=%async_computation.5 | async-start | bytes 1310720 | tf_op jit(solution)/shard_map/all_to_all | solution.py:88
  250.7 2.5 fusion.1
  253.2 1.6 constant_dynamic-slice_fusion.1
  254.8 5.4 %all-to-all-done.5 = f32[4,64,576]{2,1,0:T(8,128)} async-done(((f32[4,64,576]{2,1,0:T(8,128)}), f32[4,64,576]{2,1,0:T(8,128)}, u32[]{:S(2)}, u32[]{:S(2)}) %all-to-all-start.5) | async-done | bytes 589856 | tf_op jit(solution)/shard_map/all_to_all | solution.py:88
  260.2 1.2 fusion.10
  261.4 0.1 copy.37
  261.6 0.1 copy.36
  261.8 0.1 copy.35
  262.0 0.1 copy.34
  262.2 0.1 scatter.26
  262.3 1.5 scatter.29
  263.8 2.0 scatter.30
  265.8 2.2 scatter.31
  268.0 2.2 scatter.34
  270.2 3.7 %scatter.35 = f32[512,512]{0,1:T(8,128)S(1)} dynamic-update-slice(f32[512,512]{0,1:T(8,128)S(1)} %scatter.34, f32[64,384]{0,1:T(8,128)S(1)} %slice.247, s32[]{:T(128)} %constant.271.clone.1, s32[]{:T(128)} %constant.255.clone.1) | dynamic-update-slice | bytes 196612 | tf_op jit(solution)/shard_map/scatter | solution.py:162
  273.9 3.2 %scatter.36 = f32[512,512]{0,1:T(8,128)S(1)} dynamic-update-slice(f32[512,512]{0,1:T(8,128)S(1)} %scatter.35, f32[64,256]{0,1:T(8,128)S(1)} %slice.249, s32[]{:T(128)} %constant.272.clone.1, s32[]{:T(128)} %constant.255.clone.1) | dynamic-update-slice | bytes 131076 | tf_op jit(solution)/shard_map/scatter | solution.py:161
  277.2 3.1 scatter.39
  280.2 0.1 fusion.2
  280.4 0.3 copy.32
  280.7 0.3 bitcast_add_fusion.gram_ref
  281.0 32.5 %shard_map.67 = f32[80,512]{1,0:T(8,128)S(1)} custom-call(f32[512,512]{1,0:T(8,128)S(1)} %bitcast_add_fusion.gram_ref, f32[80,512]{1,0:T(8,128)S(1)} %copy_bitcast_fusion.w_ref), custom_call_target="tpu_custom_call" | custom-call | tf_op jit(solution)/shard_map/pallas_call | solution.py:71
  313.5 0.7 constant_dynamic-slice_fusion
  (13 shorter events, 0.1 us)
Async XLA Ops:
  7.2 65.8 %all-gather.7.cloned.1.call-start = ((), (), s32[]{:S(2)}) async-start(), calls=%async_computation.6 | async-start | bytes 4096000 | tf_op jit(solution)/shard_map/all_gather | solution.py:109
  73.0 2.3 copy-start
  78.0 42.2 %copy-start.1 = (bf16[80,128]{1,0:T(8,128)(2,1)S(1)}, bf16[80,128]{1,0:T(8,128)(2,1)}, u32[]{:S(2)}) copy-start(bf16[80,128]{1,0:T(8,128)(2,1)} %param.23) | copy-start | bytes 61444
  121.1 19.8 %all-to-all-start.3 = ((bf16[32,80,128]{2,1,0:T(8,128)(2,1)}), bf16[32,80,128]{2,1,0:T(8,128)(2,1)}, u32[]{:S(2)}, u32[]{:S(2)}) async-start(bf16[32,80,128]{2,1,0:T(8,128)(2,1)} %broadcast_in_dim.19), calls=%async_computation.3 | async-start | bytes 1310720 | tf_op jit(solution)/shard_map/all_to_all | solution.py:88
  143.5 10.8 %all-to-all-start.4 = ((f32[4,80,128]{2,1,0:T(8,128)}), f32[4,80,128]{2,1,0:T(8,128)}, u32[]{:S(2)}, u32[]{:S(2)}) async-start(f32[4,80,128]{2,1,0:T(8,128)} %broadcast_in_dim.20), calls=%async_computation.4 | async-start | bytes 327680 | tf_op jit(solution)/shard_map/all_to_all | solution.py:88
  150.3 90.0 %all-gather.9.cloned.1.call-start = ((), (), s32[]{:S(2)}) async-start(), calls=%async_computation.7 | async-start | bytes 5406720 | tf_op jit(solution)/shard_map/all_gather | solution.py:82
  174.4 69.3 %all-to-all-start.2 = ((bf16[80,32,80]{2,0,1:T(8,128)(2,1)}), bf16[80,32,80]{2,0,1:T(8,128)(2,1)}, u32[]{:S(2)}, u32[]{:S(2)}) async-start(bf16[80,32,80]{2,0,1:T(8,128)(2,1)} %copy.25), calls=%async_computation.2 | async-start | bytes 1310720 | tf_op jit(solution)/shard_map/all_to_all | solution.py:183
  245.5 14.7 %all-to-all-start.5 = ((f32[4,64,576]{2,1,0:T(8,128)}), f32[4,64,576]{2,1,0:T(8,128)}, u32[]{:S(2)}, u32[]{:S(2)}) async-start(f32[4,64,576]{2,1,0:T(8,128)} %broadcast_in_dim.21), calls=%async_computation.5 | async-start | bytes 1310720 | tf_op jit(solution)/shard_map/all_to_all | solution.py:88
Sparse Core Ops, SparseCore 0:
  27.8 45.1 all-gather.6
  156.9 83.2 all-gather.8

commit v2 on v1

v2 whole, which is shorter than its diff:
```python
import jax
import jax.numpy as jnp
from jax import lax
from jax.experimental import pallas as pl
from jax.experimental.pallas import tpu as pltpu
from jax.sharding import Mesh
from jax.sharding import PartitionSpec as P

SHARD = ("z", "yh", "x")
ROLE = ("yl", "core")
MESH = pl.DeviceIdType.MESH

smoothing = 0.95
clip_ratio = 4.0
epsilon_value = 1e-06

HIGHEST = lax.Precision.HIGHEST
NN = (((1,), (0,)), ((), ()))
TN = (((0,), (0,)), ((), ()))
NT = (((1,), (1,)), ((), ()))


def dot(a, b, dims):
    return lax.dot_general(a, b, dims, precision=HIGHEST, preferred_element_type=jnp.float32)


def bf16_dot(a, b, dims):
    return lax.dot_general(a, b, dims, preferred_element_type=jnp.float32)


def remote(src, dst, send_sem, recv_sem, **target):
    return pltpu.make_async_remote_copy(
        src_ref=src,
        dst_ref=dst,
        send_sem=send_sem,
        recv_sem=recv_sem,
        device_id=target,
        device_id_type=MESH,
    )


def arrived(ref, sem):
    pltpu.make_async_copy(ref, ref, sem).wait()


def ring(axis, step):
    return lax.rem(lax.axis_index(axis) + (4 + step), 4)


def greet(barrier, **target):
    pl.semaphore_signal(barrier, inc=1, device_id=target, device_id_type=MESH)


def gather_kernel(pay, old, out, mine, half, recv, send, recv_mine, recv_half, send_y, local_sem):
    z, yh, x = (lax.axis_index(a) for a in SHARD)
    yl, core = (lax.axis_index(a) for a in ROLE)
    role = 2 * yl + core

    barrier = pltpu.get_barrier_semaphore()
    greeted = 0
    for dh in (0, 1):
        for dl in (0, 1):
            for dc in (0, 1):
                if dh + dl + dc:
                    greet(
                        barrier,
                        yh=lax.rem(yh + dh, 2),
                        yl=lax.rem(yl + dl, 2),
                        core=lax.rem(core + dc, 2),
                    )
                    greeted += 1
    for axis in ("z", "x"):
        for step in (1, -1):
            greet(barrier, **{axis: ring(axis, step)})
            greeted += 1
    pl.semaphore_wait(barrier, greeted)

    def unit(h, k, at_z, at_x):
        return out.at[h, k, at_z, pl.ds(pl.multiple_of(at_x * 80, 16), 80), :]

    def sem(h, k, at_z, at_x):
        return recv.at[h, k, at_z * 4 + at_x]

    waits = []

    for h in (0, 1):
        first = remote(
            pay.at[h], unit(h, yl, z, x), send_y.at[h], sem(h, yl, z, x), yh=1 - yh, yl=yh
        )
        first.start()
        waits.append(first)

        @pl.when(yl == yh)
        def _():
            pltpu.make_async_copy(pay.at[h], unit(h, yl, z, x), sem(h, yl, z, x)).start()

        @pl.when(yl != yh)
        def _():
            remote(
                pay.at[h], unit(h, yl, z, x), send_y.at[2 + h], sem(h, yl, z, x), yl=yh
            ).start()

    to_partner = remote(pay, mine.at[yl], send_y.at[4], recv_mine.at[0], yl=1 - yl)
    to_partner.start()
    waits.append(to_partner)
    own_rows = pltpu.make_async_copy(pay, mine.at[yl], local_sem.at[0])
    own_rows.start()
    own_half = pltpu.make_async_copy(old.at[yl], half.at[role], local_sem.at[1])
    own_half.start()
    to_core = remote(
        old.at[yl], half.at[role], send_y.at[5], recv_half.at[role], core=1 - core
    )
    to_core.start()
    waits.append(to_core)

    counter = [0]

    def push(h, k, at_z, at_x, axis, step):
        ref = unit(h, k, at_z, at_x)
        copy = remote(
            ref, ref, send.at[counter[0]], sem(h, k, at_z, at_x), **{axis: ring(axis, step)}
        )
        counter[0] += 1
        copy.start()
        waits.append(copy)

    def place(h, first, second):
        return (second, first) if h == 0 else (first, second)

    FIRST = ("x", "z")
    SECOND = ("z", "x")
    here = {"z": z, "x": x}

    def spread(h, k, first, second):
        at_z, at_x = place(h, first, second)
        push(h, k, at_z, at_x, SECOND[h], 1)
        push(h, k, at_z, at_x, SECOND[h], -1)

    def wait_unit(h, k, first, second):
        at_z, at_x = place(h, first, second)
        arrived(unit(h, k, at_z, at_x), sem(h, k, at_z, at_x))

    def step_one(h, k, first, second, step):
        at_z, at_x = place(h, first, second)
        push(h, k, at_z, at_x, FIRST[h], step)

    for k in (0, 1):
        for h in (0, 1):
            wait_unit(h, k, here[FIRST[h]], here[SECOND[h]])
            step_one(h, k, here[FIRST[h]], here[SECOND[h]], 1)
            step_one(h, k, here[FIRST[h]], here[SECOND[h]], -1)
    for k in (0, 1):
        for h in (0, 1):
            spread(h, k, here[FIRST[h]], here[SECOND[h]])
    for k in (0, 1):
        onward = 1 if k == 0 else -1
        for h in (0, 1):
            behind = ring(FIRST[h], -onward)
            wait_unit(h, k, behind, here[SECOND[h]])
            step_one(h, k, behind, here[SECOND[h]], onward)
    for k in (0, 1):
        onward = 1 if k == 0 else -1
        for h in (0, 1):
            spread(h, k, ring(FIRST[h], -onward), here[SECOND[h]])
    for k in (0, 1):
        onward = 1 if k == 0 else -1
        for h in (0, 1):
            ahead = ring(FIRST[h], onward)
            wait_unit(h, k, ahead, here[SECOND[h]])
            spread(h, k, ahead, here[SECOND[h]])
    for k in (0, 1):
        for h in (0, 1):
            far = ring(FIRST[h], 2)
            wait_unit(h, k, far, here[SECOND[h]])
            spread(h, k, far, here[SECOND[h]])

    for dc in (0, 1):
        across = remote(
            old.at[1 - yl],
            half.at[role],
            send_y.at[6 + dc],
            recv_half.at[role],
            yl=1 - yl,
            core=lax.rem(core + dc, 2),
        )
        across.start()
        waits.append(across)

    def column(h, k, turn):
        onward = 1 if k == 0 else -1
        return ring(FIRST[h], (0, -onward, onward, 2)[turn])

    for turn in range(4):
        for k in (0, 1):
            onward = 1 if k == 0 else -1
            for h in (0, 1):
                behind = ring(SECOND[h], -onward)
                first = column(h, k, turn)
                wait_unit(h, k, first, behind)
                at_z, at_x = place(h, first, behind)
                push(h, k, at_z, at_x, SECOND[h], onward)
    for turn in range(4):
        for k in (0, 1):
            onward = 1 if k == 0 else -1
            for h in (0, 1):
                first = column(h, k, turn)
                wait_unit(h, k, first, ring(SECOND[h], onward))
                wait_unit(h, k, first, ring(SECOND[h], 2))

    own_rows.wait()
    own_half.wait()
    arrived(mine.at[1 - yl], recv_mine.at[0])
    for dl in (0, 1):
        for dc in (0, 1):
            if dl + dc:
                other = 2 * lax.rem(yl + dl, 2) + lax.rem(core + dc, 2)
                arrived(half.at[other], recv_half.at[other])
    for copy in waits:
        copy.wait_send()

    @pl.when(yl != yh)
    def _():
        for h in (0, 1):
            remote(
                pay.at[h], unit(h, yl, z, x), send_y.at[2 + h], sem(h, yl, z, x), yl=yh
            ).wait_send()


def gather(pay, old):
    return pl.pallas_call(
        gather_kernel,
        out_shape=(
            jax.ShapeDtypeStruct((2, 2, 4, 320, 384), jnp.bfloat16),
            jax.ShapeDtypeStruct((2, 2, 80, 384), jnp.bfloat16),
            jax.ShapeDtypeStruct((4, 80, 320), jnp.float32),
        ),
        in_specs=[pl.BlockSpec(memory_space=pl.ANY)] * 2,
        out_specs=(pl.BlockSpec(memory_space=pl.ANY),) * 3,
        scratch_shapes=[
            pltpu.SemaphoreType.DMA((2, 2, 16)),
            pltpu.SemaphoreType.DMA((64,)),
            pltpu.SemaphoreType.DMA((1,)),
            pltpu.SemaphoreType.DMA((4,)),
            pltpu.SemaphoreType.DMA((8,)),
            pltpu.SemaphoreType.DMA((2,)),
        ],
        compiler_params=pltpu.CompilerParams(collective_id=0, has_side_effects=True),
    )(pay, old)


def parts_of(x):
    high = x.astype(jnp.bfloat16)
    rest = x - high.astype(jnp.float32)
    middle = rest.astype(jnp.bfloat16)
    low = (rest - middle.astype(jnp.float32)).astype(jnp.bfloat16)
    return high, middle, low


def power_kernel(
    blocks, mine, half,
    gram, power, left, squares,
    partial, partial_in, stat, power_part, power_in, chunk, pieces,
    send_core, recv_core, send_sq, recv_sq, send_y, recv_y, send_w, recv_w, send_left, recv_left,
    send_rs, recv_rs, send_ag, recv_ag, send_g, recv_g,
):
    z, yh, x = (lax.axis_index(a) for a in SHARD)
    yl, core = (lax.axis_index(a) for a in ROLE)
    role = 2 * yl + core
    across = 2 * (1 - yl) + core
    shard = z * 8 + yh * 4 + x

    def peer(step):
        other = lax.rem(shard + step, 32)
        return other, {"z": other // 8, "yh": lax.rem(other // 4, 2), "x": lax.rem(other, 4)}

    barrier = pltpu.get_barrier_semaphore()

    def greet_step(step, _):
        other, place = peer(step)
        greet(barrier, **place)
        greet(barrier, yl=1 - yl, **place)
        return 0

    lax.fori_loop(1, 32, greet_step, 0)
    greet(barrier, yl=1 - yl)
    greet(barrier, core=1 - core)
    greet(barrier, yl=1 - yl, core=1 - core)

    def squares_of(i, total):
        k, at_z = i // 4, lax.rem(i, 4)

        def rows_step(j, total):
            rows = pl.ds(pl.multiple_of(j * 16, 16), 16)
            a = blocks[0, k, at_z, rows, :].astype(jnp.float32)
            b = blocks[1, k, at_z, rows, :256].astype(jnp.float32)
            a = a * a
            b = b * b
            wide = a[:, :128] + a[:, 128:256] + a[:, 256:] + b[:, :128] + b[:, 128:]
            return total + wide[:8] + wide[8:]

        return lax.fori_loop(0, 20, rows_step, total, unroll=4)

    squares[role] = lax.fori_loop(0, 8, squares_of, jnp.zeros((8, 128), jnp.float32))

    pl.semaphore_wait(barrier, 65)

    sq_copies = []
    for n, (dl, dc) in enumerate(((1, 0), (0, 1), (1, 1))):
        copy = remote(
            squares.at[role],
            squares.at[role],
            send_sq.at[n],
            recv_sq.at[role],
            yl=lax.rem(yl + dl, 2),
            core=lax.rem(core + dc, 2),
        )
        copy.start()
        sq_copies.append(copy)

    core_copies = []
    for at_z in range(4):
        total = jnp.zeros((80, 320), jnp.float32)
        for k in (0, 1):
            total += bf16_dot(mine[k, 0], blocks[0, k, at_z], NT)
            total += bf16_dot(mine[k, 1, :, :256], blocks[1, k, at_z, :, :256], NT)
        partial[at_z] = total
        copy = remote(
            partial.at[at_z],
            partial_in.at[at_z],
            send_core.at[at_z],
            recv_core.at[at_z],
            core=1 - core,
        )
        copy.start()
        core_copies.append(copy)

    for dl, dc in ((1, 0), (0, 1), (1, 1)):
        other = 2 * lax.rem(yl + dl, 2) + lax.rem(core + dc, 2)
        arrived(squares.at[other], recv_sq.at[other])
    all_squares = jnp.sum(squares[0] + squares[1] + squares[2] + squares[3])
    order_size = jnp.float32(2560)
    factor = jnp.minimum(
        1.0,
        clip_ratio
        * jnp.sqrt(order_size)
        / jnp.sqrt(jnp.full((8, 128), all_squares + epsilon_value, jnp.float32)),
    )
    weight = ((1.0 - smoothing) * (factor * factor))[:1, :1]

    sums = [jnp.zeros((80, 128), jnp.float32)] * 2
    for at_z in range(4):
        core_copies[at_z].wait_recv()
        value = smoothing * half[at_z] + weight * (partial[at_z] + partial_in[at_z])
        stat[at_z] = value
        stacked = jnp.concatenate(parts_of(value), axis=0)
        for k in (0, 1):
            product = bf16_dot(stacked, blocks[1, k, at_z, :, 256:], NN)
            sums[k] = sums[k] + (product[:80] + product[80:160] + product[160:])
    for k in (0, 1):
        power_part[k] = sums[k]
    y_copy = remote(power_part, power_in, send_y.at[0], recv_y.at[0], yl=1 - yl)
    y_copy.start()
    left[yl] = stat[role]
    left_copy = remote(stat.at[across], left.at[yl], send_left.at[0], recv_left.at[0], yl=1 - yl)
    left_copy.start()

    y_copy.wait_recv()
    w_copies = []
    for k in (0, 1):
        slot = 2 * k + core
        power[slot] = power_part[k] + power_in[k]
        copy = remote(power.at[slot], power.at[slot], send_w.at[k], recv_w.at[slot], core=1 - core)
        copy.start()
        w_copies.append(copy)
    for k in (0, 1):
        slot = 2 * k + 1 - core
        arrived(power.at[slot], recv_w.at[slot])

    columns = power[role]
    for pair in (0, 1):
        strip = dot(columns, jnp.concatenate([power[2 * pair], power[2 * pair + 1]], axis=1), TN)
        for t in range(16):
            chunk[2 * t + pair] = strip[8 * t : 8 * t + 8, :]

    def scatter_copy(step):
        other, place = peer(step)
        return remote(
            chunk.at[other], pieces.at[shard], send_rs.at[other], recv_rs.at[shard], **place
        )

    def scatter_start(step, _):
        scatter_copy(step).start()
        return 0

    lax.fori_loop(1, 32, scatter_start, 0)

    def scatter_arrive(step, total):
        other, _ = peer(step)
        arrived(pieces.at[other], recv_rs.at[other])
        return total + pieces[other]

    gram[role, shard] = lax.fori_loop(1, 32, scatter_arrive, chunk[shard])

    def spread_copy(step, flip):
        other, place = peer(step)
        if flip:
            place = dict(place, yl=1 - yl)
        return remote(
            gram.at[role, shard],
            gram.at[role, shard],
            send_ag.at[flip, other],
            recv_ag.at[flip, shard],
            **place,
        )

    def spread_start(step, _):
        spread_copy(step, 1).start()
        spread_copy(step, 0).start()
        return 0

    spread_copy(0, 1).start()
    lax.fori_loop(1, 32, spread_start, 0)

    arrived(gram.at[across, shard], recv_ag.at[1, shard])

    def spread_arrive(step, _):
        other, _ = peer(step)
        arrived(gram.at[across, other], recv_ag.at[1, other])
        arrived(gram.at[role, other], recv_ag.at[0, other])
        return 0

    lax.fori_loop(1, 32, spread_arrive, 0)

    g_copies = []
    for k in (0, 1):
        slot = 2 * k + core
        copy = remote(gram.at[slot], gram.at[slot], send_g.at[k], recv_g.at[slot], core=1 - core)
        copy.start()
        g_copies.append(copy)
    for k in (0, 1):
        slot = 2 * k + 1 - core
        arrived(gram.at[slot], recv_g.at[slot])

    arrived(left.at[1 - yl], recv_left.at[0])

    def drain(step, _):
        scatter_copy(step).wait_send()
        spread_copy(step, 1).wait_send()
        spread_copy(step, 0).wait_send()
        return 0

    lax.fori_loop(1, 32, drain, 0)
    spread_copy(0, 1).wait_send()
    for copy in sq_copies + core_copies + [y_copy, left_copy] + w_copies + g_copies:
        copy.wait_send()


def power_and_gram(blocks, mine, half):
    vmem = pl.BlockSpec(memory_space=pltpu.VMEM)
    dma = pltpu.SemaphoreType.DMA
    f32 = jnp.float32
    return pl.pallas_call(
        power_kernel,
        out_shape=(
            jax.ShapeDtypeStruct((4, 32, 8, 256), f32),
            jax.ShapeDtypeStruct((4, 80, 128), f32),
            jax.ShapeDtypeStruct((2, 80, 320), f32),
            jax.ShapeDtypeStruct((4, 8, 128), f32),
        ),
        in_specs=[vmem] * 3,
        out_specs=(vmem,) * 4,
        scratch_shapes=[
            pltpu.VMEM((4, 80, 320), f32),
            pltpu.VMEM((4, 80, 320), f32),
            pltpu.VMEM((4, 80, 320), f32),
            pltpu.VMEM((2, 80, 128), f32),
            pltpu.VMEM((2, 80, 128), f32),
            pltpu.VMEM((32, 8, 256), f32),
            pltpu.VMEM((32, 8, 256), f32),
            dma((4,)), dma((4,)),
            dma((3,)), dma((4,)),
            dma((1,)), dma((1,)),
            dma((2,)), dma((4,)),
            dma((1,)), dma((1,)),
            dma((32,)), dma((32,)),
            dma((2, 32)), dma((2, 32)),
            dma((2,)), dma((4,)),
        ],
        compiler_params=pltpu.CompilerParams(
            collective_id=1, has_side_effects=True, vmem_limit_bytes=40 << 20
        ),
    )(blocks, mine, half)


def eliminate(d_ref):
    n = d_ref.shape[0]
    sub = lax.broadcasted_iota(jnp.int32, (8, n), 0)
    lane = lax.broadcasted_iota(jnp.int32, (8, n), 1)
    for at in range(0, n, 8):
        rows = d_ref[at : at + 8, :]
        cols = [jnp.broadcast_to(rows[:, at + j : at + j + 1], (8, n)) for j in range(8)]
        inside = (lane >= at) & (lane < at + 8)
        rows = jnp.where(inside, (lane - at == sub).astype(jnp.float32), rows)
        for j in range(8):
            scale = lax.rsqrt(jnp.broadcast_to(cols[j][j : j + 1, :], (8, n)))
            below = jnp.where(sub > j, cols[j] * scale, 0.0)
            pivot = jnp.broadcast_to(rows[j : j + 1, :], (8, n)) * scale
            rows = jnp.where(sub == j, pivot, rows - below * pivot)
            for k in range(j + 1, 8):
                row = jnp.broadcast_to(cols[k][j : j + 1, :], (8, n))
                cols[k] = cols[k] - below * (row * scale)
        d_ref[at : at + 8, :] = rows
        if at + 8 < n:
            change = dot(rows, rows, TN)
            rest = d_ref[at + 8 :, :]
            lanes = lax.broadcasted_iota(jnp.int32, rest.shape, 1)
            rest = jnp.where((lanes >= at) & (lanes < at + 8), 0.0, rest)
            d_ref[at + 8 :, :] = rest - change[at + 8 :, :]


def factor_kernel(gram_ref, w_ref, q_ref, m_ref, d_ref):
    order = 512
    n = 128
    role = 2 * lax.axis_index("yl") + lax.axis_index("core")
    for r in range(4):
        for t in range(16):
            for pair in (0, 1):
                at = n * r + 8 * t
                m_ref[at : at + 8, 256 * pair : 256 * pair + 256] = gram_ref[r, 2 * t + pair]
        m_ref[order:, n * r : n * r + n] = w_ref[r]
    row = lax.broadcasted_iota(jnp.int32, (n, n), 0)
    col = lax.broadcasted_iota(jnp.int32, (n, n), 1)
    for at in range(0, order, n):
        end = at + n
        d_ref[...] = m_ref[at:end, at:end]
        eliminate(d_ref)
        inverse = jnp.where(col <= row, d_ref[...], 0.0)
        panel = dot(m_ref[end:, at:end], inverse, NT)

        @pl.when(role == at // n)
        def _():
            q_ref[...] = panel[order - end :, :]

        if end < order:
            m_ref[end:, end:] = m_ref[end:, end:] - dot(panel, panel[: order - end, :], NT)


def factor(gram, power):
    return pl.pallas_call(
        factor_kernel,
        out_shape=jax.ShapeDtypeStruct((80, 128), jnp.float32),
        in_specs=[pl.BlockSpec(memory_space=pltpu.VMEM)] * 2,
        out_specs=pl.BlockSpec(memory_space=pltpu.VMEM),
        scratch_shapes=[pltpu.VMEM((592, 512), jnp.float32), pltpu.VMEM((128, 128), jnp.float32)],
        compiler_params=pltpu.CompilerParams(vmem_limit_bytes=32 << 20),
        cost_estimate=pl.CostEstimate(
            flops=20_000_000_000, bytes_accessed=1_500_000, transcendentals=0
        ),
    )(gram, power)


def on_device(gradient, left_old, right_old, basis_old):
    z, yh, x = (lax.axis_index(a) for a in SHARD)
    yl, core = (lax.axis_index(a) for a in ROLE)
    pay = jnp.stack(
        [gradient[:, :384], jnp.concatenate([gradient[:, 384:], basis_old], axis=1)]
    )
    old = jnp.stack([left_old[:, :320], left_old[:, 320:]])
    blocks, mine, half = gather(pay, old)
    gram, power, left, squares = power_and_gram(blocks, mine, half)
    left_basis = factor(gram, power)
    left_stat = jnp.concatenate([left[0], left[1]], axis=1)

    columns = jnp.concatenate(
        [blocks[0].reshape(2, 1280, 384), blocks[1].reshape(2, 1280, 384)[:, :, :256]], axis=2
    )
    kept = lax.dynamic_index_in_dim(columns, z // 2, 0, keepdims=False)
    kept = lax.dynamic_slice_in_dim(kept, 80 * (4 * yh + x), 80, 1)
    swapped = lax.ppermute(kept, "core", [(0, 1), (1, 0)])
    kept = jnp.where(core == lax.rem(z, 2), kept, swapped)
    right = lax.dot_general(
        kept, columns, (((0,), (1,)), ((), ())), preferred_element_type=jnp.float32
    )
    theirs = lax.dynamic_index_in_dim(right, 1 - yl, 1, keepdims=False)
    ours = lax.dynamic_index_in_dim(right, yl, 1, keepdims=False)
    right_gram = ours + lax.ppermute(theirs, "yl", [(0, 1), (1, 0)])
    total = jnp.sum(squares)
    factor_now = jnp.minimum(
        1.0, clip_ratio * jnp.sqrt(jnp.float32(2560)) / jnp.sqrt(total + epsilon_value)
    )
    right_stat = smoothing * right_old + (1.0 - smoothing) * (factor_now * factor_now) * right_gram
    return (left_stat, right_stat, left_basis)


def solution(mesh):
    finer = Mesh(mesh.devices.reshape(2, 2, 4, 2, 4), ("yl", "core", "z", "yh", "x"))
    return jax.shard_map(
        on_device,
        mesh=finer,
        in_specs=(P(SHARD, ROLE),) * 4,
        out_specs=(P(SHARD, ROLE),) * 3,
        check_vma=False,
    )
```

time: 322 us -> 130 us (0.40)
  blocking collectives: 113 us -> 0 us
  waiting for transfers between devices: 82.2 us -> 3.93 us
  Pallas kernels: 32.5 us -> 106 us
  local copies, waits for them, and re-layouts: 37.9 us -> 8.55 us
  starting transfers between devices: 24.2 us -> 1.69 us
  between operations: 15 us -> 1.45 us
  matrix products: 7.38 us -> 1.72 us
  other arithmetic: 9.28 us -> 5.72 us
    pallas_call x1 -> x3, Pallas kernels: 32.5 us -> 106 us  [the longest x1 37.8 us: power_and_gram(): pl.pallas_call(power_kernel, out_shape=(jax.ShapeDtypeStruct((4, 32, 8, 2...]
    all_gather x2 -> x0, waiting for transfers between devices: 63.7 us -> none  [the longest x1 61.3 us: over_pieces(): parts = lax.all_gather(x, axis)]
    all_to_all x2 -> x0, blocking collectives: 54 us -> none  [copy_for_each(): lax.all_to_all(jnp.broadcast_to(x[None], (size, *x.shape)), axis, 0, 0, t...]
    psum x5 -> x0, blocking collectives: 38 us -> none  [by_axis(): return functools.reduce(lax.psum, axes, x)]
    all_to_all x4 -> x0, starting transfers between devices: 24.2 us -> none  [the longest x3 19.5 us: copy_for_each(): lax.all_to_all(jnp.broadcast_to(x[None], (size, *x.shape)), axis, 0, 0, t...]
    all_gather x2 -> x0, blocking collectives: 20.5 us -> none  [all_blocks(): parts = lax.all_gather(parts, axes[k])]
    all_to_all x4 -> x0, waiting for transfers between devices: 18.5 us -> none  [the longest x3 18.5 us: copy_for_each(): lax.all_to_all(jnp.broadcast_to(x[None], (size, *x.shape)), axis, 0, 0, t...]
    scatter x8 -> x0, local copies, waits for them, and re-layouts: 18 us -> none  [the longest x4 10.4 us: lower_gram(): lower_part.at[other * tile_size:(other + 1) * tile_size, :tail]]
  transfers between devices with their start and end apart: 6 -> 2, of which waited for: 5 -> 1; matrix products, arithmetic and copies ran while one was open for 6% -> 1% of each run, Pallas kernels for 0% -> 55%
where the time goes in v2:
time: 130 us; the launch traced here: 129 us
  Pallas kernels  106 us (82%)
  local copies, waits for them, and re-layouts  8.55 us (7%)
  other arithmetic  5.72 us (4%)
  waiting for transfers between devices  3.93 us (3%)
  matrix products  1.72 us (1%)
  starting transfers between devices  1.69 us (1%)
  between operations  1.45 us (1%)
    pallas_call x1, Pallas kernels, power_and_gram(): pl.pallas_call(power_kernel, out_shape=(jax.ShapeDtypeStruct((4, 32, 8, 2...  37.8 us
    pallas_call x1, Pallas kernels, gather(): pl.pallas_call(gather_kernel, out_shape=(jax.ShapeDtypeStruct((2, 2, 4, 3...  35.2 us
    pallas_call x1, Pallas kernels, factor(): pl.pallas_call(factor_kernel, out_shape=jax.ShapeDtypeStruct((80, 128), j...  33.5 us
    ppermute x1, waiting for transfers between devices, on_device(): right_gram = ours + lax.ppermute(theirs, 'yl', [(0, 1), (1, 0)])  3.93 us
  transfers between devices with their start and end apart: 2, of which 1 were waited for; matrix products, arithmetic and copies ran while one was open for 1% of the time, Pallas kernels for 55%

profile of v2, /device:TPU:1, one launch (start us, length us, event | category | flops | bytes accessed | tf_op | source)
XLA Modules:
  0.0 129.4 jit_solution(4364877155671153327)
XLA Ops:
  0.7 0.8 slice.28
  1.4 1.1 slice_bitcast_fusion.3
  2.5 0.9 maximum_bitcast_fusion
  3.4 0.7 pad_maximum_fusion.4.pay
  4.0 0.7 pad_maximum_fusion.2.old
  4.8 35.2 %shard_map.67 = (bf16[2,2,4,320,384]{4,3,2,1,0:T(8,128)(2,1)}, bf16[2,2,80,384]{3,2,1,0:T(8,128)(2,1)}, f32[4,80,320]{2,1,0:T(8,128)}) custom-call(bf16[2,80,384]{2,1,0:T(8,128)(2,1)} %pad_maximum_fusion.4.pay, f32[2,80,320]{2,1,0:T(8,128)} %pad_maximum_fusion.2.old), custom_call_target="tpu_custom_call" | custom-call | tf_op jit(solution)/shard_map/pallas_call | solution.py:230
  39.9 2.5 %fusion.9 = (bf16[1,2,4,320,384]{4,3,2,1,0:T(8,128)(2,1)S(1)}, bf16[1,2,4,320,384]{4,3,2,1,0:T(8,128)(2,1)S(1)}) fusion(bf16[2,2,4,320,384]{4,3,2,1,0:T(8,128)(2,1)} %get-tuple-element.10.blocks), kind=kLoop, calls=%fused_computation.23 | loop fusion | bytes 7864320 | tf_op jit(solution)/shard_map/slice | solution.py:575
  42.5 0.0 copy-start.1
  42.5 0.0 copy-start.2
  42.5 1.1 slice.36
  43.6 0.4 fusion.1
  44.0 0.8 copy.7
  44.8 0.9 collective-permute-start
  45.7 0.0 copy-done.1
  45.7 0.0 copy-done.2
  45.7 0.0 copy-start
  45.7 2.1 %copy-done = bf16[2,2,4,320,384]{4,3,2,1,0:T(8,128)(2,1)S(1)} copy-done((bf16[2,2,4,320,384]{4,3,2,1,0:T(8,128)(2,1)S(1)}, bf16[2,2,4,320,384]{4,3,2,1,0:T(8,128)(2,1)}, u32[]{:S(2)}) %copy-start) | copy-done | bytes 3932184
  47.8 37.8 %shard_map.68 = (f32[4,32,8,256]{3,2,1,0:T(8,128)S(1)}, f32[4,80,128]{2,1,0:T(8,128)S(1)}, f32[2,80,320]{2,1,0:T(8,128)S(1)}, f32[4,8,128]{2,1,0:T(8,128)S(1)}) custom-call(bf16[2,2,4,320,384]{4,3,2,1,0:T(8,128)(2,1)S(1)} %copy-done, bf16[2,2,80,384]{3,2,1,0:T(8,128)(2,1)S(1)} %copy-done.2, f32[4,80,320]{2,1,0:T(8,128)S(1)} %copy-done.1), custom_call_target="tpu_custom_call" | custom-call | tf_op jit(solution)/shard_map/pallas_call | solution.py:462
  85.6 0.0 copy-start.3
  85.6 33.5 %shard_map.69 = f32[80,128]{1,0:T(8,128)} custom-call(f32[4,32,8,256]{3,2,1,0:T(8,128)S(1)} %get-tuple-element.15.gram_ref, f32[4,80,128]{2,1,0:T(8,128)S(1)} %get-tuple-element.16.w_ref), custom_call_target="tpu_custom_call" | custom-call | flops 20000000000 | bytes 1500000 | tf_op jit(solution)/shard_map/pallas_call | solution.py:549
  119.1 0.0 collective-permute-done
  119.1 0.0 copy-done.3
  119.1 1.7 %fusion = f32[80,2,640]{2,0,1:T(8,128)S(1)} fusion(bf16[2,1280,256]{2,1,0:T(8,128)(2,1)S(1)} %copy-done.3, bf16[2,1280,384]{2,1,0:T(8,128)(2,1)S(1)} %bitcast.31, bf16[1280,80]{0,1:T(8,128)(2,1)} %collective-permute-done, pred[]{:T(512)S(6)} %eq.3, bf16[1,1280,80]{1,2,0:T(8,128)(2,1)} %copy.7), kind=kOutput, calls=%fused_computation.3 | convolution fusion | flops 268800000 | bytes 4096001 | tf_op jit(solution)/shard_map/dot_general | solution.py:581
  120.8 0.0 copy-start.4
  120.8 0.8 collective-permute-start.1
  121.7 0.0 copy-done.4
  121.7 0.6 reduce_sum.9
  123.0 0.8 pad_maximum_fusion.3
  123.8 3.9 %collective-permute-done.1 = f32[80,640]{1,0:T(8,128)S(1)} collective-permute-done((f32[80,640]{1,0:T(8,128)S(1)}, f32[80,640]{1,0:T(8,128)S(1)}, u32[]{:S(2)}, u32[]{:S(2)}) %collective-permute-start.1) | collective-permute-done | bytes 204832 | tf_op jit(solution)/shard_map/ppermute | solution.py:586
  127.7 1.7 %fusion.3 = f32[80,640]{1,0:T(8,128)} fusion(f32[80,640]{1,0:T(8,128)S(1)} %collective-permute-done.1, f32[80,2,640]{2,0,1:T(8,128)} %copy-done.4, s32[]{:T(128)S(6)} %select_n.38, f32[80,640]{1,0:T(8,128)} %param.6, f32[]{:T(128)S(6)} %mul_shard_map.9), kind=kLoop, calls=%fused_computation.9 | loop fusion | flops 204800 | bytes 819208 | tf_op jit(solution)/shard_map/add | solution.py:591
  (2 shorter events, 0.0 us)
Async XLA Ops:
  42.5 3.2 %copy-start.1 = (f32[4,80,320]{2,1,0:T(8,128)S(1)}, f32[4,80,320]{2,1,0:T(8,128)}, u32[]{:S(2)}) copy-start(f32[4,80,320]{2,1,0:T(8,128)} %get-tuple-element.12.half) | copy-start | bytes 1228804
  42.5 3.2 %copy-start.2 = (bf16[2,2,80,384]{3,2,1,0:T(8,128)(2,1)S(1)}, bf16[2,2,80,384]{3,2,1,0:T(8,128)(2,1)}, u32[]{:S(2)}) copy-start(bf16[2,2,80,384]{3,2,1,0:T(8,128)(2,1)} %get-tuple-element.11.mine) | copy-start | bytes 737284
  44.8 74.2 %collective-permute-start = (bf16[1280,80]{0,1:T(8,128)(2,1)}, bf16[1280,80]{0,1:T(8,128)(2,1)}, u32[]{:S(2)}, u32[]{:S(2)}) collective-permute-start(bf16[1280,80]{0,1:T(8,128)(2,1)} %bitcast.8), channel_id=1, source_target_pairs={{0,32},{32,0},{1,33},{33,1},{2,34},{34,2},{3,35},{35,3},{4,36},{36... | collective-permute-start | bytes 614408 | tf_op jit(solution)/shard_map/ppermute | solution.py:579
  45.7 2.1 %copy-start = (bf16[2,2,4,320,384]{4,3,2,1,0:T(8,128)(2,1)S(1)}, bf16[2,2,4,320,384]{4,3,2,1,0:T(8,128)(2,1)}, u32[]{:S(2)}) copy-start(bf16[2,2,4,320,384]{4,3,2,1,0:T(8,128)(2,1)} %get-tuple-element.10.blocks) | copy-start | bytes 11796484
  85.6 33.5 %copy-start.3 = (bf16[2,1280,256]{2,1,0:T(8,128)(2,1)S(1)}, bf16[2,1280,256]{2,1,0:T(8,128)(2,1)}, u32[]{:S(2)}) copy-start(bf16[2,1280,256]{2,1,0:T(8,128)(2,1)} %slice.36) | copy-start | bytes 3932164
  120.8 0.9 copy-start.4
  120.8 6.8 %collective-permute-start.1 = (f32[80,640]{1,0:T(8,128)S(1)}, f32[80,640]{1,0:T(8,128)S(1)}, u32[]{:S(2)}, u32[]{:S(2)}) collective-permute-start(f32[80,640]{1,0:T(8,128)S(1)} %dynamic-slice_bitcast_fusion), channel_id=1, source_target_pairs={{0,64},{64,0},{1,65},{65,1},{2,66},{66,2},{3,67},{67,3},{4,68},{68... | collective-permute-start | bytes 614408 | tf_op jit(solution)/shard_map/ppermute | solution.py:586

commit v3 on v2

v3 whole, which is shorter than its diff:
```python
import jax
import jax.numpy as jnp
from jax import lax
from jax.experimental import pallas as pl
from jax.experimental.pallas import tpu as pltpu
from jax.sharding import Mesh
from jax.sharding import PartitionSpec as P

SHARD = ("z", "yh", "x")
ROLE = ("yl", "core")
MESH = pl.DeviceIdType.MESH

smoothing = 0.95
clip_ratio = 4.0
epsilon_value = 1e-06

NN = (((1,), (0,)), ((), ()))
TN = (((0,), (0,)), ((), ()))
NT = (((1,), (1,)), ((), ()))


def bf16_dot(a, b, dims):
    return lax.dot_general(a, b, dims, preferred_element_type=jnp.float32)


def remote(src, dst, send_sem, recv_sem, **target):
    return pltpu.make_async_remote_copy(
        src_ref=src,
        dst_ref=dst,
        send_sem=send_sem,
        recv_sem=recv_sem,
        device_id=target,
        device_id_type=MESH,
    )


def arrived(ref, sem):
    pltpu.make_async_copy(ref, ref, sem).wait()


def ring(axis, step):
    return lax.rem(lax.axis_index(axis) + (4 + step), 4)


def greet(barrier, **target):
    pl.semaphore_signal(barrier, inc=1, device_id=target, device_id_type=MESH)


def stat_weight(squares):
    full = jnp.full((8, 128), squares + epsilon_value, jnp.float32)
    factor = jnp.minimum(1.0, clip_ratio * jnp.sqrt(jnp.float32(2560)) / jnp.sqrt(full))
    return (1.0 - smoothing) * (factor * factor)


def parts_of(x):
    high = x.astype(jnp.bfloat16)
    rest = x - high.astype(jnp.float32)
    middle = rest.astype(jnp.bfloat16)
    low = (rest - middle.astype(jnp.float32)).astype(jnp.bfloat16)
    return high, middle, low


def full_dot(a, b, dims):
    a_axis, b_axis = dims[0][0][0], dims[0][1][0]
    ah, am, al = parts_of(a)
    bh, bm, bl = (ah, am, al) if b is a else parts_of(b)
    left = jnp.concatenate([ah, ah, am, ah, al, am], axis=a_axis)
    right = jnp.concatenate([bh, bm, bh, bl, bh, bm], axis=b_axis)
    return bf16_dot(left, right, dims)


def main_kernel(
    gradient, basis, left_old,
    gram, power, left, squares, ours, theirs,
    blocks, mine, half, sq_sum, kept, right_out, partial, partial_in, stat, power_part, power_in, chunk, pieces,
    give, recv, send, send_y, recv_mine, recv_half, local_sem,
    send_core, recv_core, send_sq, recv_sq, send_w, recv_w, send_one, recv_one,
    send_rs, recv_rs, send_ag, recv_ag, send_g, recv_g,
):
    z, yh, x = (lax.axis_index(a) for a in SHARD)
    yl, core = (lax.axis_index(a) for a in ROLE)
    role = 2 * yl + core
    across = 2 * (1 - yl) + core
    shard = z * 8 + yh * 4 + x

    def peer(step):
        other = lax.rem(shard + step, 32)
        return other, {"z": other // 8, "yh": lax.rem(other // 4, 2), "x": lax.rem(other, 4)}

    barrier = pltpu.get_barrier_semaphore()

    def greet_step(step, _):
        other, place = peer(step)
        greet(barrier, **place)
        greet(barrier, yl=1 - yl, **place)
        return 0

    greet(barrier, yl=1 - yl)
    greet(barrier, core=1 - core)
    greet(barrier, yl=1 - yl, core=1 - core)
    lax.fori_loop(1, 32, greet_step, 0)

    own_rows = pltpu.make_async_copy(gradient, mine.at[yl], local_sem.at[0])
    own_rows.start()
    own_half = pltpu.make_async_copy(
        left_old.at[:, pl.ds(pl.multiple_of(256 * yl, 128), 384)], half.at[role], local_sem.at[1]
    )
    own_half.start()
    sq_sum[...] = jnp.zeros((8, 128), jnp.float32)
    waits = []

    pl.semaphore_wait(barrier, 65)

    def unit(h, k, at_z, at_x):
        return blocks.at[h, k, at_z, pl.ds(pl.multiple_of(at_x * 80, 16), 80), :]

    def sem(h, k, at_z, at_x):
        return recv.at[h, k, at_z * 4 + at_x]

    def pieces_of(h):
        to = unit(h, yl, z, x)
        if h == 0:
            return [(gradient.at[:, :384], to)]
        return [(gradient.at[:, 384:], to.at[:, :256]), (basis, to.at[:, 256:])]

    def give_copy(h, n, src, dst):
        return remote(src, dst, give.at[0, h + n], sem(h, yl, z, x), yh=1 - yh, yl=yh)

    def lend_copy(h, n, src, dst):
        return remote(src, dst, give.at[1, h + n], sem(h, yl, z, x), yl=yh)

    for h in (0, 1):
        for n, (src, dst) in enumerate(pieces_of(h)):
            copy = give_copy(h, n, src, dst)
            copy.start()
            waits.append(copy)

            @pl.when(yl == yh)
            def _():
                pltpu.make_async_copy(src, dst, sem(h, yl, z, x)).start()

            @pl.when(yl != yh)
            def _():
                lend_copy(h, n, src, dst).start()

    to_partner = remote(gradient, mine.at[yl], send_y.at[0], recv_mine.at[0], yl=1 - yl)
    to_partner.start()
    waits.append(to_partner)
    to_core = remote(
        left_old.at[:, pl.ds(pl.multiple_of(256 * yl, 128), 384)],
        half.at[role],
        send_y.at[1],
        recv_half.at[role],
        core=1 - core,
    )
    to_core.start()
    waits.append(to_core)

    counter = [0]

    def push(h, k, at_z, at_x, axis, step):
        ref = unit(h, k, at_z, at_x)
        copy = remote(
            ref, ref, send.at[counter[0]], sem(h, k, at_z, at_x), **{axis: ring(axis, step)}
        )
        counter[0] += 1
        copy.start()
        waits.append(copy)

    def place(h, first, second):
        return (second, first) if h == 0 else (first, second)

    FIRST = ("x", "z")
    SECOND = ("z", "x")
    here = {"z": z, "x": x}

    def spread(h, k, first, second):
        at_z, at_x = place(h, first, second)
        push(h, k, at_z, at_x, SECOND[h], 1)
        push(h, k, at_z, at_x, SECOND[h], -1)

    def wait_unit(h, k, first, second):
        at_z, at_x = place(h, first, second)
        arrived(unit(h, k, at_z, at_x), sem(h, k, at_z, at_x))

    def add_squares(h, k, first, second):
        at_z, at_x = place(h, first, second)
        width = 384 if h == 0 else 256
        start = pl.multiple_of(at_x * 80, 16)
        value = blocks[h, k, at_z, pl.ds(start, 80), :width].astype(jnp.float32)
        value = value * value
        wide = value[:, :128]
        for lane in range(128, width, 128):
            wide = wide + value[:, lane : lane + 128]
        total = wide[:8]
        for row in range(8, 80, 8):
            total = total + wide[row : row + 8]
        sq_sum[...] += total

    def step_one(h, k, first, second, step):
        at_z, at_x = place(h, first, second)
        push(h, k, at_z, at_x, FIRST[h], step)

    both = [(k, h, 1 if k == 0 else -1) for k in (0, 1) for h in (0, 1)]

    for k, h, onward in both:
        wait_unit(h, k, here[FIRST[h]], here[SECOND[h]])
        step_one(h, k, here[FIRST[h]], here[SECOND[h]], 1)
        step_one(h, k, here[FIRST[h]], here[SECOND[h]], -1)
    for k, h, onward in both:
        spread(h, k, here[FIRST[h]], here[SECOND[h]])
    for k, h, onward in both:
        add_squares(h, k, here[FIRST[h]], here[SECOND[h]])
    for k, h, onward in both:
        behind = ring(FIRST[h], -onward)
        wait_unit(h, k, behind, here[SECOND[h]])
        step_one(h, k, behind, here[SECOND[h]], onward)
    for k, h, onward in both:
        spread(h, k, ring(FIRST[h], -onward), here[SECOND[h]])
    for k, h, onward in both:
        ahead = ring(FIRST[h], onward)
        wait_unit(h, k, ahead, here[SECOND[h]])
        spread(h, k, ahead, here[SECOND[h]])
    for k, h, onward in both:
        add_squares(h, k, ring(FIRST[h], -onward), here[SECOND[h]])
        add_squares(h, k, ring(FIRST[h], onward), here[SECOND[h]])
    for k, h, onward in both:
        far = ring(FIRST[h], 2)
        wait_unit(h, k, far, here[SECOND[h]])
        spread(h, k, far, here[SECOND[h]])

    for dc in (0, 1):
        over = remote(
            left_old.at[:, pl.ds(pl.multiple_of(256 * (1 - yl), 128), 384)],
            half.at[role],
            send_y.at[2 + dc],
            recv_half.at[role],
            yl=1 - yl,
            core=lax.rem(core + dc, 2),
        )
        over.start()
        waits.append(over)
    for k, h, onward in both:
        add_squares(h, k, ring(FIRST[h], 2), here[SECOND[h]])

    def column(h, k, turn):
        onward = 1 if k == 0 else -1
        return ring(FIRST[h], (0, -onward, onward, 2)[turn])

    for turn in range(4):
        for k, h, onward in both:
            behind = ring(SECOND[h], -onward)
            first = column(h, k, turn)
            wait_unit(h, k, first, behind)
            at_z, at_x = place(h, first, behind)
            push(h, k, at_z, at_x, SECOND[h], onward)
        for k, h, onward in both:
            add_squares(h, k, column(h, k, turn), ring(SECOND[h], -onward))
    for turn in range(4):
        for k, h, onward in both:
            first = column(h, k, turn)
            ahead, far = ring(SECOND[h], onward), ring(SECOND[h], 2)
            wait_unit(h, k, first, ahead)
            add_squares(h, k, first, ahead)
            wait_unit(h, k, first, far)
            add_squares(h, k, first, far)
    own_rows.wait()
    arrived(mine.at[1 - yl], recv_mine.at[0])

    squares[role] = sq_sum[...]
    sq_copies = []
    for n, (dl, dc) in enumerate(((1, 0), (0, 1), (1, 1))):
        copy = remote(
            squares.at[role],
            squares.at[role],
            send_sq.at[n],
            recv_sq.at[role],
            yl=lax.rem(yl + dl, 2),
            core=lax.rem(core + dc, 2),
        )
        copy.start()
        sq_copies.append(copy)
    core_copies = []
    for at_z in range(4):
        total = jnp.zeros((80, 320), jnp.float32)
        for k in (0, 1):
            total += bf16_dot(mine[k, :, :384], blocks[0, k, at_z], NT)
            total += bf16_dot(mine[k, :, 384:], blocks[1, k, at_z, :, :256], NT)
        partial[at_z] = total
        copy = remote(
            partial.at[at_z],
            partial_in.at[at_z],
            send_core.at[at_z],
            recv_core.at[at_z],
            core=1 - core,
        )
        copy.start()
        core_copies.append(copy)

    own_half.wait()
    for dl, dc in ((0, 1), (1, 0), (1, 1)):
        other = 2 * lax.rem(yl + dl, 2) + lax.rem(core + dc, 2)
        arrived(half.at[other], recv_half.at[other])
        arrived(squares.at[other], recv_sq.at[other])
    all_squares = jnp.sum(squares[0] + squares[1] + squares[2] + squares[3])
    weight = stat_weight(all_squares)[:1, :1]

    sums = [jnp.zeros((80, 128), jnp.float32)] * 2
    for at_z in range(4):
        core_copies[at_z].wait_recv()
        held = half[at_z]
        held = jnp.where(yl == 0, held[:, :320], held[:, 64:])
        value = smoothing * held + weight * (partial[at_z] + partial_in[at_z])
        stat[at_z] = value
        stacked = jnp.concatenate(parts_of(value), axis=0)
        for k in (0, 1):
            product = bf16_dot(stacked, blocks[1, k, at_z, :, 256:], NN)
            sums[k] = sums[k] + (product[:80] + product[80:160] + product[160:])
    for k in (0, 1):
        power_part[k] = sums[k]
    y_copy = remote(power_part, power_in, send_one.at[0], recv_one.at[0], yl=1 - yl)
    y_copy.start()
    left[yl] = stat[role]
    left_copy = remote(stat.at[across], left.at[yl], send_one.at[1], recv_one.at[1], yl=1 - yl)
    left_copy.start()

    has_columns = core == lax.rem(z, 2)
    kept_copy = remote(kept, kept, send_one.at[2], recv_one.at[2], core=1 - core)

    @pl.when(has_columns)
    def _():
        offset = 80 * (4 * yh + x)
        row = lax.broadcasted_iota(jnp.int32, (80, 640), 0)
        col = lax.broadcasted_iota(jnp.int32, (80, 640), 1)
        pick = jnp.where(col == row + offset, 1.0, 0.0).astype(jnp.bfloat16)
        for at_z in range(4):
            chosen = bf16_dot(pick[:, :384], blocks[0, z // 2, at_z], NT)
            chosen += bf16_dot(pick[:, 384:], blocks[1, z // 2, at_z, :, :256], NT)
            kept[at_z] = chosen.astype(jnp.bfloat16)
        kept_copy.start()

    y_copy.wait_recv()
    w_copies = []
    for k in (0, 1):
        slot = 2 * k + core
        power[slot] = power_part[k] + power_in[k]
        copy = remote(power.at[slot], power.at[slot], send_w.at[k], recv_w.at[slot], core=1 - core)
        copy.start()
        w_copies.append(copy)
    for k in (0, 1):
        slot = 2 * k + 1 - core
        arrived(power.at[slot], recv_w.at[slot])

    columns = power[role]
    for pair in (0, 1):
        strip = full_dot(columns, jnp.concatenate([power[2 * pair], power[2 * pair + 1]], axis=1), TN)
        for t in range(16):
            chunk[2 * t + pair] = strip[8 * t : 8 * t + 8, :]

    def scatter_copy(step):
        other, place = peer(step)
        return remote(
            chunk.at[other], pieces.at[shard], send_rs.at[other], recv_rs.at[shard], **place
        )

    def scatter_start(step, _):
        scatter_copy(step).start()
        return 0

    lax.fori_loop(1, 32, scatter_start, 0)

    @pl.when(jnp.logical_not(has_columns))
    def _():
        arrived(kept, recv_one.at[2])

    def right_product(k, out):
        for h, width in ((0, 384), (1, 256)):
            total = jnp.zeros((80, width), jnp.float32)
            for at_z in range(4):
                total += bf16_dot(kept[at_z], blocks[h, k, at_z, :, :width], NN)
            out[:, 384 * h : 384 * h + width] = total

    right_product(1 - yl, right_out)
    right_copy = remote(right_out, theirs, send_one.at[3], recv_one.at[3], yl=1 - yl)
    right_copy.start()

    def scatter_arrive(step, total):
        other, _ = peer(step)
        arrived(pieces.at[other], recv_rs.at[other])
        return total + pieces[other]

    gram[role, shard] = lax.fori_loop(1, 32, scatter_arrive, chunk[shard])

    def spread_copy(step, flip):
        other, place = peer(step)
        if flip:
            place = dict(place, yl=1 - yl)
        return remote(
            gram.at[role, shard],
            gram.at[role, shard],
            send_ag.at[flip, other],
            recv_ag.at[flip, shard],
            **place,
        )

    def spread_start(step, _):
        spread_copy(step, 1).start()
        spread_copy(step, 0).start()
        return 0

    spread_copy(0, 1).start()
    lax.fori_loop(1, 32, spread_start, 0)
    right_product(yl, ours)

    arrived(gram.at[across, shard], recv_ag.at[1, shard])

    def spread_arrive(step, _):
        other, _ = peer(step)
        arrived(gram.at[across, other], recv_ag.at[1, other])
        arrived(gram.at[role, other], recv_ag.at[0, other])
        return 0

    lax.fori_loop(1, 32, spread_arrive, 0)

    g_copies = []
    for k in (0, 1):
        slot = 2 * k + core
        copy = remote(gram.at[slot], gram.at[slot], send_g.at[k], recv_g.at[slot], core=1 - core)
        copy.start()
        g_copies.append(copy)
    for k in (0, 1):
        slot = 2 * k + 1 - core
        arrived(gram.at[slot], recv_g.at[slot])

    arrived(left.at[1 - yl], recv_one.at[1])
    arrived(theirs, recv_one.at[3])

    @pl.when(has_columns)
    def _():
        kept_copy.wait_send()

    def drain(step, _):
        scatter_copy(step).wait_send()
        spread_copy(step, 1).wait_send()
        spread_copy(step, 0).wait_send()
        return 0

    lax.fori_loop(1, 32, drain, 0)
    spread_copy(0, 1).wait_send()
    for copy in sq_copies + core_copies + [y_copy, left_copy, right_copy] + w_copies + g_copies:
        copy.wait_send()
    for copy in waits:
        copy.wait_send()

    @pl.when(yl != yh)
    def _():
        for h in (0, 1):
            for n, (src, dst) in enumerate(pieces_of(h)):
                lend_copy(h, n, src, dst).wait_send()


def gather_and_power(gradient, basis, left_old):
    any_space = pl.BlockSpec(memory_space=pl.ANY)
    vmem = pl.BlockSpec(memory_space=pltpu.VMEM)
    dma = pltpu.SemaphoreType.DMA
    f32, bf16 = jnp.float32, jnp.bfloat16
    return pl.pallas_call(
        main_kernel,
        out_shape=(
            jax.ShapeDtypeStruct((4, 32, 8, 256), f32),
            jax.ShapeDtypeStruct((4, 80, 128), f32),
            jax.ShapeDtypeStruct((2, 80, 320), f32),
            jax.ShapeDtypeStruct((4, 8, 128), f32),
            jax.ShapeDtypeStruct((80, 640), f32),
            jax.ShapeDtypeStruct((80, 640), f32),
        ),
        in_specs=[any_space] * 3,
        out_specs=(vmem,) * 6,
        scratch_shapes=[
            pltpu.VMEM((2, 2, 4, 320, 384), bf16),
            pltpu.VMEM((2, 80, 640), bf16),
            pltpu.VMEM((4, 80, 384), f32),
            pltpu.VMEM((8, 128), f32),
            pltpu.VMEM((4, 80, 320), bf16),
            pltpu.VMEM((80, 640), f32),
            pltpu.VMEM((4, 80, 320), f32),
            pltpu.VMEM((4, 80, 320), f32),
            pltpu.VMEM((4, 80, 320), f32),
            pltpu.VMEM((2, 80, 128), f32),
            pltpu.VMEM((2, 80, 128), f32),
            pltpu.VMEM((32, 8, 256), f32),
            pltpu.VMEM((32, 8, 256), f32),
            dma((2, 3)), dma((2, 2, 16)), dma((64,)), dma((4,)), dma((1,)), dma((4,)), dma((2,)),
            dma((4,)), dma((4,)),
            dma((3,)), dma((4,)),
            dma((2,)), dma((4,)),
            dma((4,)), dma((4,)),
            dma((32,)), dma((32,)),
            dma((2, 32)), dma((2, 32)),
            dma((2,)), dma((4,)),
        ],
        compiler_params=pltpu.CompilerParams(
            collective_id=0, has_side_effects=True, vmem_limit_bytes=48 << 20
        ),
    )(gradient, basis, left_old)


def eliminate(block):
    n = 128
    sub = lax.broadcasted_iota(jnp.int32, (8, n), 0)
    lane = lax.broadcasted_iota(jnp.int32, (8, n), 1)
    m = [block[at : at + 8, :] for at in range(0, n, 8)]
    for b in range(n // 8):
        at = 8 * b
        inside = (lane >= at) & (lane < at + 8)

        def columns_of(v):
            return [jnp.broadcast_to(v[:, at + j : at + j + 1], (8, n)) for j in range(8)]

        rows = m[b]
        cols = columns_of(rows)
        rows = jnp.where(inside, (lane - at == sub).astype(jnp.float32), rows)
        more = b + 1 < n // 8
        if more:
            next_rows = m[b + 1]
            next_cols = columns_of(next_rows)
            next_rows = jnp.where(inside, 0.0, next_rows)
        for j in range(8):
            scale = lax.rsqrt(jnp.broadcast_to(cols[j][j : j + 1, :], (8, n)))
            below = jnp.where(sub > j, cols[j] * scale, 0.0)
            pivot = jnp.broadcast_to(rows[j : j + 1, :], (8, n)) * scale
            rows = jnp.where(sub == j, pivot, rows - below * pivot)
            if more:
                next_below = next_cols[j] * scale
                next_rows = next_rows - next_below * pivot
            for k in range(j + 1, 8):
                row = jnp.broadcast_to(cols[k][j : j + 1, :], (8, n)) * scale
                cols[k] = cols[k] - below * row
                if more:
                    next_cols[k] = next_cols[k] - next_below * row
        m[b] = rows
        if more:
            m[b + 1] = next_rows
        if b + 2 < n // 8:
            change = full_dot(rows, rows, TN)
            for i in range(b + 2, n // 8):
                m[i] = jnp.where(inside, 0.0, m[i]) - change[8 * i : 8 * i + 8, :]
    return jnp.concatenate(m, axis=0)


def factor_kernel(
    gram_ref, w_ref, left_ref, sq_ref, ours_ref, theirs_ref, right_old_ref,
    left_stat_ref, right_stat_ref, q_ref, m_ref,
):
    order = 512
    n = 128
    role = 2 * lax.axis_index("yl") + lax.axis_index("core")
    weight = stat_weight(jnp.sum(sq_ref[0] + sq_ref[1] + sq_ref[2] + sq_ref[3]))[:1, :1]
    left_stat_ref[:, :320] = left_ref[0]
    left_stat_ref[:, 320:] = left_ref[1]
    right_stat_ref[...] = smoothing * right_old_ref[...] + weight * (ours_ref[...] + theirs_ref[...])
    for r in range(4):
        for t in range(16):
            for pair in (0, 1):
                at = n * r + 8 * t
                m_ref[at : at + 8, 256 * pair : 256 * pair + 256] = gram_ref[r, 2 * t + pair]
        m_ref[order:, n * r : n * r + n] = w_ref[r]
    row = lax.broadcasted_iota(jnp.int32, (n, n), 0)
    col = lax.broadcasted_iota(jnp.int32, (n, n), 1)
    for at in range(0, order, n):
        end = at + n
        inverse = jnp.where(col <= row, eliminate(m_ref[at:end, at:end]), 0.0)
        panel = full_dot(m_ref[end:, at:end], inverse, NT)

        @pl.when(role == at // n)
        def _():
            q_ref[...] = panel[order - end :, :]

        if end < order:
            m_ref[end:, end:] = m_ref[end:, end:] - full_dot(panel, panel[: order - end, :], NT)


def factor(gram, power, left, squares, ours, theirs, right_old):
    return pl.pallas_call(
        factor_kernel,
        out_shape=(
            jax.ShapeDtypeStruct((80, 640), jnp.float32),
            jax.ShapeDtypeStruct((80, 640), jnp.float32),
            jax.ShapeDtypeStruct((80, 128), jnp.float32),
        ),
        in_specs=[pl.BlockSpec(memory_space=pltpu.VMEM)] * 7,
        out_specs=(pl.BlockSpec(memory_space=pltpu.VMEM),) * 3,
        scratch_shapes=[pltpu.VMEM((592, 512), jnp.float32)],
        compiler_params=pltpu.CompilerParams(vmem_limit_bytes=32 << 20),
    )(gram, power, left, squares, ours, theirs, right_old)


def on_device(gradient, left_old, right_old, basis_old):
    gathered = gather_and_power(gradient, basis_old, left_old)
    return factor(*gathered, right_old)


def solution(mesh):
    finer = Mesh(mesh.devices.reshape(2, 2, 4, 2, 4), ("yl", "core", "z", "yh", "x"))
    return jax.shard_map(
        on_device,
        mesh=finer,
        in_specs=(P(SHARD, ROLE),) * 4,
        out_specs=(P(SHARD, ROLE),) * 3,
        check_vma=False,
    )
```

time: 130 us -> 91.9 us (0.71)
  Pallas kernels: 106 us -> 88.5 us
  local copies, waits for them, and re-layouts: 8.55 us -> 2.55 us
  other arithmetic: 5.72 us -> 0 us
  waiting for transfers between devices: 3.93 us -> 0 us
  matrix products: 1.72 us -> 0 us
  starting transfers between devices: 1.69 us -> 0 us
    pallas_call x3 -> x2, Pallas kernels: 106 us -> 88.5 us  [the longest x1 69.7 us: gather_and_power(): pl.pallas_call(main_kernel, out_shape=(jax.ShapeDtypeStruct((4, 32, 8, 25...]
    slice x3 -> x0, local copies, waits for them, and re-layouts: 4.47 us -> none  [the longest x1 2.55 us: on_device(): blocks[0].reshape(2, 1280, 384)]
    ppermute x2 -> x0, waiting for transfers between devices: 3.93 us -> none  [the longest x1 3.93 us: on_device(): right_gram = ours + lax.ppermute(theirs, 'yl', [(0, 1), (1, 0)])]
    another operation x3 -> x0, other arithmetic: 2.24 us -> none  [the longest x2 1.53 us: on_device(): jnp.stack([gradient[:, :384], jnp.concatenate([gradient[:, 384:], basis_o...]
    add x1 -> x0, other arithmetic: 1.74 us -> none  [on_device(): smoothing * right_old]
    dot_general x1 -> x0, matrix products: 1.72 us -> none  [on_device(): lax.dot_general(kept, columns, (((0,), (1,)), ((), ())), preferred_elemen...]
    ppermute x2 -> x0, starting transfers between devices: 1.69 us -> none  [the longest x1 0.87 us: on_device(): swapped = lax.ppermute(kept, 'core', [(0, 1), (1, 0)])]
  transfers between devices with their start and end apart: 2 -> 0, of which waited for: 1 -> 0; matrix products, arithmetic and copies ran while one was open for 1% -> 0% of each run, Pallas kernels for 55% -> 0%
where the time goes in v3:
time: 91.9 us; the launch traced here: 91.7 us
  Pallas kernels  88.5 us (96%)
  local copies, waits for them, and re-layouts  2.55 us (3%)
    pallas_call x1, Pallas kernels, gather_and_power(): pl.pallas_call(main_kernel, out_shape=(jax.ShapeDtypeStruct((4, 32, 8, 25...  69.7 us
    pallas_call x1, Pallas kernels, factor(): pl.pallas_call(factor_kernel, out_shape=(jax.ShapeDtypeStruct((80, 640),...  18.8 us
    unnamed x8, local copies, waits for them, and re-layouts  2.55 us

profile of v3, /device:TPU:1, one launch (start us, length us, event | category | flops | bytes accessed | tf_op | source)
XLA Modules:
  0.0 91.7 jit_solution(3408220245666903168)
XLA Ops:
  0.6 0.0 copy-start
  0.6 0.9 %copy-done = f32[80,640]{1,0:T(8,128)S(1)} copy-done((f32[80,640]{1,0:T(8,128)S(1)}, f32[80,640]{1,0:T(8,128)}, u32[]{:S(2)}) %copy-start) | copy-done | bytes 204824
  1.6 0.0 copy-start.2
  1.6 0.9 copy-done.2
  2.5 0.0 copy-start.3
  2.5 0.7 copy-done.3
  3.2 0.0 copy-start.1
  3.2 69.7 %shard_map.67 = (f32[4,32,8,256]{3,2,1,0:T(8,128)S(1)}, f32[4,80,128]{2,1,0:T(8,128)S(1)}, f32[2,80,320]{2,1,0:T(8,128)S(1)}, f32[4,8,128]{2,1,0:T(8,128)S(1)}, ...) custom-call(bf16[80,640]{1,0:T(8,128)(2,1)S(1)} %copy-done.2, bf16[80,128]{1,0:T(8,128)(2,1)S(1)} %copy-done.3, ...), custom_call_target="tpu_custom_call" | custom-call | tf_op jit(solution)/shard_map/pallas_call | solution.py:467
  72.9 0.0 copy-done.1
  72.9 18.8 %shard_map.68 = (f32[80,640]{1,0:T(8,128)}, f32[80,640]{1,0:T(8,128)}, f32[80,128]{1,0:T(8,128)}) custom-call(f32[4,32,8,256]{3,2,1,0:T(8,128)S(1)} %get-tuple-element.9.gram_ref, f32[4,80,128]{2,1,0:T(8,128)S(1)} %get-tuple-element.10.w_ref, f32[2,80,320]{2,1,0:T(8,128)S(1)} %get-tuple-element.11.left_ref, f32[4,8,128]{2,1,0:T(8,128)S(1)} %get-tuple-element.12.sq_ref, ...), custom_call_target="tpu_custom_call" | custom-call | tf_op jit(solution)/shard_map/pallas_call | solution.py:584
Async XLA Ops:
  0.6 0.9 %copy-start = (f32[80,640]{1,0:T(8,128)S(1)}, f32[80,640]{1,0:T(8,128)}, u32[]{:S(2)}) copy-start(f32[80,640]{1,0:T(8,128)} %left_old.1) | copy-start | bytes 614404
  1.6 0.9 copy-start.2
  2.5 0.7 copy-start.3
  3.2 69.7 %copy-start.1 = (f32[80,640]{1,0:T(8,128)S(1)}, f32[80,640]{1,0:T(8,128)}, u32[]{:S(2)}) copy-start(f32[80,640]{1,0:T(8,128)} %right_old_ref.1) | copy-start | bytes 614404

commit v4 on v3

--- a/solution.py
+++ b/solution.py
@@ -83,22 +83,31 @@
     across = 2 * (1 - yl) + core
     shard = z * 8 + yh * 4 + x
 
-    def peer(step):
-        other = lax.rem(shard + step, 32)
-        return other, {"z": other // 8, "yh": lax.rem(other // 4, 2), "x": lax.rem(other, 4)}
+    group = lax.rem(yl + yh, 2)
+    strip_at = 2 * group + core
+    strip_over = 2 * (1 - group) + core
+
+    def peer(turn):
+        at_z = lax.rem(z + 2 + turn // 8, 4)
+        at_x = lax.rem(x + 2 + lax.rem(turn, 4), 4)
+        at_yh = lax.rem(yh + 1 + lax.rem(turn // 4, 2), 2)
+        at_yl = lax.rem(group + at_yh, 2)
+        return at_z * 8 + at_yh * 4 + at_x, {"z": at_z, "yh": at_yh, "x": at_x, "yl": at_yl}
+
+    def over_peers(body, init):
+        return lax.fori_loop(23, 32, body, lax.fori_loop(0, 22, body, init))
 
     barrier = pltpu.get_barrier_semaphore()
-
-    def greet_step(step, _):
-        other, place = peer(step)
-        greet(barrier, **place)
-        greet(barrier, yl=1 - yl, **place)
-        return 0
-
-    greet(barrier, yl=1 - yl)
-    greet(barrier, core=1 - core)
-    greet(barrier, yl=1 - yl, core=1 - core)
-    lax.fori_loop(1, 32, greet_step, 0)
+    for dh, dl, dc in ((0, 0, 1), (0, 1, 0), (0, 1, 1), (1, 0, 0), (1, 1, 0)):
+        greet(
+            barrier,
+            yh=lax.rem(yh + dh, 2),
+            yl=lax.rem(yl + dl, 2),
+            core=lax.rem(core + dc, 2),
+        )
+    for axis in ("z", "x"):
+        for step in (1, -1):
+            greet(barrier, **{axis: ring(axis, step)})
 
     own_rows = pltpu.make_async_copy(gradient, mine.at[yl], local_sem.at[0])
     own_rows.start()
@@ -109,7 +118,7 @@
     sq_sum[...] = jnp.zeros((8, 128), jnp.float32)
     waits = []
 
-    pl.semaphore_wait(barrier, 65)
+    pl.semaphore_wait(barrier, 9)
 
     def unit(h, k, at_z, at_x):
         return blocks.at[h, k, at_z, pl.ds(pl.multiple_of(at_x * 80, 16), 80), :]
@@ -142,19 +151,6 @@
             @pl.when(yl != yh)
             def _():
                 lend_copy(h, n, src, dst).start()
-
-    to_partner = remote(gradient, mine.at[yl], send_y.at[0], recv_mine.at[0], yl=1 - yl)
-    to_partner.start()
-    waits.append(to_partner)
-    to_core = remote(
-        left_old.at[:, pl.ds(pl.multiple_of(256 * yl, 128), 384)],
-        half.at[role],
-        send_y.at[1],
-        recv_half.at[role],
-        core=1 - core,
-    )
-    to_core.start()
-    waits.append(to_core)
 
     counter = [0]
 
@@ -174,10 +170,10 @@
     SECOND = ("z", "x")
     here = {"z": z, "x": x}
 
-    def spread(h, k, first, second):
+    def spread(h, k, onward, first, second):
         at_z, at_x = place(h, first, second)
-        push(h, k, at_z, at_x, SECOND[h], 1)
-        push(h, k, at_z, at_x, SECOND[h], -1)
+        push(h, k, at_z, at_x, SECOND[h], onward)
+        push(h, k, at_z, at_x, SECOND[h], -onward)
 
     def wait_unit(h, k, first, second):
         at_z, at_x = place(h, first, second)
@@ -201,14 +197,28 @@
         at_z, at_x = place(h, first, second)
         push(h, k, at_z, at_x, FIRST[h], step)
 
-    both = [(k, h, 1 if k == 0 else -1) for k in (0, 1) for h in (0, 1)]
+    both = [(k, h, onward) for k, onward in ((yh, 1), (1 - yh, -1)) for h in (0, 1)]
 
     for k, h, onward in both:
         wait_unit(h, k, here[FIRST[h]], here[SECOND[h]])
-        step_one(h, k, here[FIRST[h]], here[SECOND[h]], 1)
-        step_one(h, k, here[FIRST[h]], here[SECOND[h]], -1)
-    for k, h, onward in both:
-        spread(h, k, here[FIRST[h]], here[SECOND[h]])
+        step_one(h, k, here[FIRST[h]], here[SECOND[h]], onward)
+        step_one(h, k, here[FIRST[h]], here[SECOND[h]], -onward)
+    for toward in (1, -1):
+        for k, h, onward in both:
+            at_z, at_x = place(h, here[FIRST[h]], here[SECOND[h]])
+            push(h, k, at_z, at_x, SECOND[h], toward * onward)
+    to_partner = remote(gradient, mine.at[yl], send_y.at[0], recv_mine.at[0], yl=1 - yl)
+    to_partner.start()
+    waits.append(to_partner)
+    to_core = remote(
+        left_old.at[:, pl.ds(pl.multiple_of(256 * yl, 128), 384)],
+        half.at[role],
+        send_y.at[1],
+        recv_half.at[role],
+        core=1 - core,
+    )
+    to_core.start()
+    waits.append(to_core)
     for k, h, onward in both:
         add_squares(h, k, here[FIRST[h]], here[SECOND[h]])
     for k, h, onward in both:
@@ -216,18 +226,18 @@
         wait_unit(h, k, behind, here[SECOND[h]])
         step_one(h, k, behind, here[SECOND[h]], onward)
     for k, h, onward in both:
-        spread(h, k, ring(FIRST[h], -onward), here[SECOND[h]])
+        spread(h, k, onward, ring(FIRST[h], -onward), here[SECOND[h]])
     for k, h, onward in both:
         ahead = ring(FIRST[h], onward)
         wait_unit(h, k, ahead, here[SECOND[h]])
-        spread(h, k, ahead, here[SECOND[h]])
+        spread(h, k, onward, ahead, here[SECOND[h]])
     for k, h, onward in both:
         add_squares(h, k, ring(FIRST[h], -onward), here[SECOND[h]])
         add_squares(h, k, ring(FIRST[h], onward), here[SECOND[h]])
     for k, h, onward in both:
         far = ring(FIRST[h], 2)
         wait_unit(h, k, far, here[SECOND[h]])
-        spread(h, k, far, here[SECOND[h]])
+        spread(h, k, onward, far, here[SECOND[h]])
 
     for dc in (0, 1):
         over = remote(
@@ -243,22 +253,28 @@
     for k, h, onward in both:
         add_squares(h, k, ring(FIRST[h], 2), here[SECOND[h]])
 
-    def column(h, k, turn):
-        onward = 1 if k == 0 else -1
+    def column(h, onward, turn):
         return ring(FIRST[h], (0, -onward, onward, 2)[turn])
 
     for turn in range(4):
         for k, h, onward in both:
             behind = ring(SECOND[h], -onward)
-            first = column(h, k, turn)
+            first = column(h, onward, turn)
             wait_unit(h, k, first, behind)
             at_z, at_x = place(h, first, behind)
             push(h, k, at_z, at_x, SECOND[h], onward)
         for k, h, onward in both:
-            add_squares(h, k, column(h, k, turn), ring(SECOND[h], -onward))
+            add_squares(h, k, column(h, onward, turn), ring(SECOND[h], -onward))
+    own_half.wait()
+    for dl, dc in ((0, 1), (1, 0), (1, 1)):
+        other = 2 * lax.rem(yl + dl, 2) + lax.rem(core + dc, 2)
+        arrived(half.at[other], recv_half.at[other])
+    for at_z in range(4):
+        held = half[at_z]
+        stat[at_z] = smoothing * jnp.where(yl == 0, held[:, :320], held[:, 64:])
     for turn in range(4):
         for k, h, onward in both:
-            first = column(h, k, turn)
+            first = column(h, onward, turn)
             ahead, far = ring(SECOND[h], onward), ring(SECOND[h], 2)
             wait_unit(h, k, first, ahead)
             add_squares(h, k, first, ahead)
@@ -297,10 +313,8 @@
         copy.start()
         core_copies.append(copy)
 
-    own_half.wait()
     for dl, dc in ((0, 1), (1, 0), (1, 1)):
         other = 2 * lax.rem(yl + dl, 2) + lax.rem(core + dc, 2)
-        arrived(half.at[other], recv_half.at[other])
         arrived(squares.at[other], recv_sq.at[other])
     all_squares = jnp.sum(squares[0] + squares[1] + squares[2] + squares[3])
     weight = stat_weight(all_squares)[:1, :1]
@@ -308,9 +322,7 @@
     sums = [jnp.zeros((80, 128), jnp.float32)] * 2
     for at_z in range(4):
         core_copies[at_z].wait_recv()
-        held = half[at_z]
-        held = jnp.where(yl == 0, held[:, :320], held[:, 64:])
-        value = smoothing * held + weight * (partial[at_z] + partial_in[at_z])
+        value = stat[at_z] + weight * (partial[at_z] + partial_in[at_z])
         stat[at_z] = value
         stacked = jnp.concatenate(parts_of(value), axis=0)
         for k in (0, 1):
@@ -351,23 +363,23 @@
         slot = 2 * k + 1 - core
         arrived(power.at[slot], recv_w.at[slot])
 
-    columns = power[role]
+    columns = power[strip_at]
     for pair in (0, 1):
         strip = full_dot(columns, jnp.concatenate([power[2 * pair], power[2 * pair + 1]], axis=1), TN)
         for t in range(16):
             chunk[2 * t + pair] = strip[8 * t : 8 * t + 8, :]
 
-    def scatter_copy(step):
-        other, place = peer(step)
+    def scatter_copy(turn):
+        other, place = peer(turn)
         return remote(
             chunk.at[other], pieces.at[shard], send_rs.at[other], recv_rs.at[shard], **place
         )
 
-    def scatter_start(step, _):
-        scatter_copy(step).start()
+    def scatter_start(turn, _):
+        scatter_copy(turn).start()
         return 0
 
-    lax.fori_loop(1, 32, scatter_start, 0)
+    over_peers(scatter_start, 0)
 
     @pl.when(jnp.logical_not(has_columns))
     def _():
@@ -384,43 +396,42 @@
     right_copy = remote(right_out, theirs, send_one.at[3], recv_one.at[3], yl=1 - yl)
     right_copy.start()
 
-    def scatter_arrive(step, total):
-        other, _ = peer(step)
+    def scatter_arrive(turn, total):
+        other, _ = peer(turn)
         arrived(pieces.at[other], recv_rs.at[other])
         return total + pieces[other]
 
-    gram[role, shard] = lax.fori_loop(1, 32, scatter_arrive, chunk[shard])
-
-    def spread_copy(step, flip):
-        other, place = peer(step)
+    gram[strip_at, shard] = over_peers(scatter_arrive, chunk[shard])
+
+    def spread_copy(turn, flip):
+        other, place = peer(turn)
         if flip:
-            place = dict(place, yl=1 - yl)
+            place = dict(place, yl=1 - place["yl"])
         return remote(
-            gram.at[role, shard],
-            gram.at[role, shard],
+            gram.at[strip_at, shard],
+            gram.at[strip_at, shard],
             send_ag.at[flip, other],
             recv_ag.at[flip, shard],
             **place,
         )
 
-    def spread_start(step, _):
-        spread_copy(step, 1).start()
-        spread_copy(step, 0).start()
+    def spread_start(turn, _):
+        spread_copy(turn, 1).start()
+        spread_copy(turn, 0).start()
         return 0
 
-    spread_copy(0, 1).start()
-    lax.fori_loop(1, 32, spread_start, 0)
+    over_peers(spread_start, 0)
+    spread_copy(22, 1).start()
     right_product(yl, ours)
 
-    arrived(gram.at[across, shard], recv_ag.at[1, shard])
-
-    def spread_arrive(step, _):
-        other, _ = peer(step)
-        arrived(gram.at[across, other], recv_ag.at[1, other])
-        arrived(gram.at[role, other], recv_ag.at[0, other])
+    def spread_arrive(turn, _):
+        other, _ = peer(turn)
+        arrived(gram.at[strip_over, other], recv_ag.at[1, other])
+        arrived(gram.at[strip_at, other], recv_ag.at[0, other])
         return 0
 
-    lax.fori_loop(1, 32, spread_arrive, 0)
+    arrived(gram.at[strip_over, shard], recv_ag.at[1, shard])
+    over_peers(spread_arrive, 0)
 
     g_copies = []
     for k in (0, 1):
@@ -439,14 +450,14 @@
     def _():
         kept_copy.wait_send()
 
-    def drain(step, _):
-        scatter_copy(step).wait_send()
-        spread_copy(step, 1).wait_send()
-        spread_copy(step, 0).wait_send()
+    def drain(turn, _):
+        scatter_copy(turn).wait_send()
+        spread_copy(turn, 1).wait_send()
+        spread_copy(turn, 0).wait_send()
         return 0
 
-    lax.fori_loop(1, 32, drain, 0)
-    spread_copy(0, 1).wait_send()
+    over_peers(drain, 0)
+    spread_copy(22, 1).wait_send()
     for copy in sq_copies + core_copies + [y_copy, left_copy, right_copy] + w_copies + g_copies:
         copy.wait_send()
     for copy in waits:
@@ -510,37 +521,48 @@
     sub = lax.broadcasted_iota(jnp.int32, (8, n), 0)
     lane = lax.broadcasted_iota(jnp.int32, (8, n), 1)
     m = [block[at : at + 8, :] for at in range(0, n, 8)]
+
+    def columns_of(v, at):
+        return [jnp.broadcast_to(v[:, at + j : at + j + 1], (8, n)) for j in range(8)]
+
+    def row_of(v, j):
+        return jnp.broadcast_to(v[j : j + 1, :], (8, n))
+
+    cols = columns_of(m[0], 0)
     for b in range(n // 8):
         at = 8 * b
         inside = (lane >= at) & (lane < at + 8)
-
-        def columns_of(v):
-            return [jnp.broadcast_to(v[:, at + j : at + j + 1], (8, n)) for j in range(8)]
-
         rows = m[b]
-        cols = columns_of(rows)
-        rows = jnp.where(inside, (lane - at == sub).astype(jnp.float32), rows)
         more = b + 1 < n // 8
         if more:
             next_rows = m[b + 1]
-            next_cols = columns_of(next_rows)
+            next_cols = columns_of(next_rows, at)
+            later = columns_of(rows, at + 8)
+            next_later = columns_of(next_rows, at + 8)
             next_rows = jnp.where(inside, 0.0, next_rows)
+        rows = jnp.where(inside, (lane - at == sub).astype(jnp.float32), rows)
         for j in range(8):
-            scale = lax.rsqrt(jnp.broadcast_to(cols[j][j : j + 1, :], (8, n)))
+            scale = lax.rsqrt(row_of(cols[j], j))
             below = jnp.where(sub > j, cols[j] * scale, 0.0)
-            pivot = jnp.broadcast_to(rows[j : j + 1, :], (8, n)) * scale
+            pivot = row_of(rows, j) * scale
             rows = jnp.where(sub == j, pivot, rows - below * pivot)
             if more:
                 next_below = next_cols[j] * scale
                 next_rows = next_rows - next_below * pivot
             for k in range(j + 1, 8):
-                row = jnp.broadcast_to(cols[k][j : j + 1, :], (8, n)) * scale
+                row = row_of(cols[k], j) * scale
                 cols[k] = cols[k] - below * row
                 if more:
                     next_cols[k] = next_cols[k] - next_below * row
+            if more:
+                for k in range(8):
+                    row = row_of(later[k], j) * scale
+                    later[k] = later[k] - below * row
+                    next_later[k] = next_later[k] - next_below * row
         m[b] = rows
         if more:
             m[b + 1] = next_rows
+            cols = next_later
         if b + 2 < n // 8:
             change = full_dot(rows, rows, TN)
             for i in range(b + 2, n // 8):

time: 91.9 us -> 88.7 us (0.965)
  Pallas kernels: 88.5 us -> 85.3 us
    pallas_call x1, Pallas kernels: 69.7 us -> 67.9 us  [gather_and_power(): pl.pallas_call(main_kernel, out_shape=(jax.ShapeDtypeStruct((4, 32, 8, 25...]
    pallas_call x1, Pallas kernels: 18.8 us -> 17.4 us  [factor(): pl.pallas_call(factor_kernel, out_shape=(jax.ShapeDtypeStruct((80, 640),...]
where the time goes in v4:
time: 88.7 us; the launch traced here: 88.5 us
  Pallas kernels  85.3 us (96%)
  local copies, waits for them, and re-layouts  2.55 us (3%)
    pallas_call x1, Pallas kernels, gather_and_power(): pl.pallas_call(main_kernel, out_shape=(jax.ShapeDtypeStruct((4, 32, 8, 25...  67.9 us
    pallas_call x1, Pallas kernels, factor(): pl.pallas_call(factor_kernel, out_shape=(jax.ShapeDtypeStruct((80, 640),...  17.4 us
    unnamed x8, local copies, waits for them, and re-layouts  2.55 us

profile of v4, /device:TPU:1, one launch (start us, length us, event | category | flops | bytes accessed | tf_op | source)
XLA Modules:
  0.0 88.5 jit_solution(159753020445401492)
XLA Ops:
  0.6 0.0 copy-start
  0.6 0.9 %copy-done = f32[80,640]{1,0:T(8,128)S(1)} copy-done((f32[80,640]{1,0:T(8,128)S(1)}, f32[80,640]{1,0:T(8,128)}, u32[]{:S(2)}) %copy-start) | copy-done | bytes 204824
  1.6 0.0 copy-start.2
  1.6 0.9 %copy-done.2 = bf16[80,640]{1,0:T(8,128)(2,1)S(1)} copy-done((bf16[80,640]{1,0:T(8,128)(2,1)S(1)}, bf16[80,640]{1,0:T(8,128)(2,1)}, u32[]{:S(2)}) %copy-start.2) | copy-done | bytes 102424
  2.5 0.0 copy-start.3
  2.5 0.7 copy-done.3
  3.2 0.0 copy-start.1
  3.2 67.9 %shard_map.67 = (f32[4,32,8,256]{3,2,1,0:T(8,128)S(1)}, f32[4,80,128]{2,1,0:T(8,128)S(1)}, f32[2,80,320]{2,1,0:T(8,128)S(1)}, f32[4,8,128]{2,1,0:T(8,128)S(1)}, ...) custom-call(bf16[80,640]{1,0:T(8,128)(2,1)S(1)} %copy-done.2, bf16[80,128]{1,0:T(8,128)(2,1)S(1)} %copy-done.3, ...), custom_call_target="tpu_custom_call" | custom-call | tf_op jit(solution)/shard_map/pallas_call | solution.py:478
  71.1 0.0 copy-done.1
  71.1 17.4 %shard_map.68 = (f32[80,640]{1,0:T(8,128)}, f32[80,640]{1,0:T(8,128)}, f32[80,128]{1,0:T(8,128)}) custom-call(f32[4,32,8,256]{3,2,1,0:T(8,128)S(1)} %get-tuple-element.9.gram_ref, f32[4,80,128]{2,1,0:T(8,128)S(1)} %get-tuple-element.10.w_ref, f32[2,80,320]{2,1,0:T(8,128)S(1)} %get-tuple-element.11.left_ref, f32[4,8,128]{2,1,0:T(8,128)S(1)} %get-tuple-element.12.sq_ref, ...), custom_call_target="tpu_custom_call" | custom-call | tf_op jit(solution)/shard_map/pallas_call | solution.py:606
Async XLA Ops:
  0.6 0.9 %copy-start = (f32[80,640]{1,0:T(8,128)S(1)}, f32[80,640]{1,0:T(8,128)}, u32[]{:S(2)}) copy-start(f32[80,640]{1,0:T(8,128)} %left_old.1) | copy-start | bytes 614404
  1.6 0.9 %copy-start.2 = (bf16[80,640]{1,0:T(8,128)(2,1)S(1)}, bf16[80,640]{1,0:T(8,128)(2,1)}, u32[]{:S(2)}) copy-start(bf16[80,640]{1,0:T(8,128)(2,1)} %gradient.1) | copy-start | bytes 307204
  2.5 0.7 copy-start.3
  3.2 67.9 %copy-start.1 = (f32[80,640]{1,0:T(8,128)S(1)}, f32[80,640]{1,0:T(8,128)}, u32[]{:S(2)}) copy-start(f32[80,640]{1,0:T(8,128)} %right_old_ref.1) | copy-start | bytes 614404

commit v5 on v4

--- a/solution.py
+++ b/solution.py
@@ -363,20 +363,41 @@
         slot = 2 * k + 1 - core
         arrived(power.at[slot], recv_w.at[slot])
 
-    columns = power[strip_at]
-    for pair in (0, 1):
-        strip = full_dot(columns, jnp.concatenate([power[2 * pair], power[2 * pair + 1]], axis=1), TN)
+    def block(a, b):
+        return full_dot(power[a], power[b], TN)
+
+    half_row = lax.rem(strip_at, 2)
+    thirds = (
+        block(strip_at, strip_at),
+        block(jnp.minimum(strip_at + 1, 3), lax.rem(strip_at, 3)),
+        block(2 + half_row, half_row),
+    )
+    for n in (0, 1):
         for t in range(16):
-            chunk[2 * t + pair] = strip[8 * t : 8 * t + 8, :]
-
-    def scatter_copy(turn):
+            chunk[16 * n + t] = thirds[n][8 * t : 8 * t + 8]
+    lower_half = jnp.where(strip_at < 2, thirds[2][:64], thirds[2][64:])
+    for t in range(8):
+        chunk[32 + t] = lower_half[8 * t : 8 * t + 8]
+    doubled = shard < 8
+
+    def scatter_copy(turn, more):
         other, place = peer(turn)
-        return remote(
-            chunk.at[other], pieces.at[shard], send_rs.at[other], recv_rs.at[shard], **place
+        return other, remote(
+            chunk.at[32 * more + other],
+            pieces.at[more, shard],
+            send_rs.at[more, other],
+            recv_rs.at[more, shard],
+            **place,
         )
 
     def scatter_start(turn, _):
-        scatter_copy(turn).start()
+        other, copy = scatter_copy(turn, 0)
+        copy.start()
+
+        @pl.when(other < 8)
+        def _():
+            scatter_copy(turn, 1)[1].start()
+
         return 0
 
     over_peers(scatter_start, 0)
@@ -398,39 +419,57 @@
 
     def scatter_arrive(turn, total):
         other, _ = peer(turn)
-        arrived(pieces.at[other], recv_rs.at[other])
-        return total + pieces[other]
-
-    gram[strip_at, shard] = over_peers(scatter_arrive, chunk[shard])
-
-    def spread_copy(turn, flip):
+        arrived(pieces.at[0, other], recv_rs.at[0, other])
+        return total + pieces[0, other]
+
+    def scatter_arrive_more(turn, total):
+        other, _ = peer(turn)
+        arrived(pieces.at[1, other], recv_rs.at[1, other])
+        return total + pieces[1, other]
+
+    def spread_copy(turn, flip, more):
         other, place = peer(turn)
         if flip:
             place = dict(place, yl=1 - place["yl"])
+        tile = gram.at[strip_at, 32 * more + shard]
         return remote(
-            gram.at[strip_at, shard],
-            gram.at[strip_at, shard],
-            send_ag.at[flip, other],
-            recv_ag.at[flip, shard],
-            **place,
+            tile, tile, send_ag.at[flip, more, other], recv_ag.at[flip, more, shard], **place
         )
 
-    def spread_start(turn, _):
-        spread_copy(turn, 1).start()
-        spread_copy(turn, 0).start()
-        return 0
-
-    over_peers(spread_start, 0)
-    spread_copy(22, 1).start()
+    def spread_all(more):
+        def spread_start(turn, _):
+            spread_copy(turn, 1, more).start()
+            spread_copy(turn, 0, more).start()
+            return 0
+
+        over_peers(spread_start, 0)
+        spread_copy(22, 1, more).start()
+
+    gram[strip_at, shard] = over_peers(scatter_arrive, chunk[shard])
+    spread_all(0)
+
+    @pl.when(doubled)
+    def _():
+        gram[strip_at, 32 + shard] = over_peers(scatter_arrive_more, chunk[32 + shard])
+        spread_all(1)
+
     right_product(yl, ours)
+
+    def tile_arrives(flip, other):
+        strip = strip_over if flip else strip_at
+        arrived(gram.at[strip, other], recv_ag.at[flip, 0, other])
+
+        @pl.when(other < 8)
+        def _():
+            arrived(gram.at[strip, 32 + other], recv_ag.at[flip, 1, other])
 
     def spread_arrive(turn, _):
         other, _ = peer(turn)
-        arrived(gram.at[strip_over, other], recv_ag.at[1, other])
-        arrived(gram.at[strip_at, other], recv_ag.at[0, other])
+        tile_arrives(1, other)
+        tile_arrives(0, other)
         return 0
 
-    arrived(gram.at[strip_over, shard], recv_ag.at[1, shard])
+    tile_arrives(1, shard)
     over_peers(spread_arrive, 0)
 
     g_copies = []
@@ -451,13 +490,29 @@
         kept_copy.wait_send()
 
     def drain(turn, _):
-        scatter_copy(turn).wait_send()
-        spread_copy(turn, 1).wait_send()
-        spread_copy(turn, 0).wait_send()
+        other, copy = scatter_copy(turn, 0)
+        copy.wait_send()
+        spread_copy(turn, 1, 0).wait_send()
+        spread_copy(turn, 0, 0).wait_send()
+
+        @pl.when(other < 8)
+        def _():
+            scatter_copy(turn, 1)[1].wait_send()
+
+        @pl.when(doubled)
+        def _():
+            spread_copy(turn, 1, 1).wait_send()
+            spread_copy(turn, 0, 1).wait_send()
+
         return 0
 
     over_peers(drain, 0)
-    spread_copy(22, 1).wait_send()
+    spread_copy(22, 1, 0).wait_send()
+
+    @pl.when(doubled)
+    def _():
+        spread_copy(22, 1, 1).wait_send()
+
     for copy in sq_copies + core_copies + [y_copy, left_copy, right_copy] + w_copies + g_copies:
         copy.wait_send()
     for copy in waits:
@@ -478,7 +533,7 @@
     return pl.pallas_call(
         main_kernel,
         out_shape=(
-            jax.ShapeDtypeStruct((4, 32, 8, 256), f32),
+            jax.ShapeDtypeStruct((4, 40, 8, 128), f32),
             jax.ShapeDtypeStruct((4, 80, 128), f32),
             jax.ShapeDtypeStruct((2, 80, 320), f32),
             jax.ShapeDtypeStruct((4, 8, 128), f32),
@@ -499,15 +554,15 @@
             pltpu.VMEM((4, 80, 320), f32),
             pltpu.VMEM((2, 80, 128), f32),
             pltpu.VMEM((2, 80, 128), f32),
-            pltpu.VMEM((32, 8, 256), f32),
-            pltpu.VMEM((32, 8, 256), f32),
+            pltpu.VMEM((40, 8, 128), f32),
+            pltpu.VMEM((2, 32, 8, 128), f32),
             dma((2, 3)), dma((2, 2, 16)), dma((64,)), dma((4,)), dma((1,)), dma((4,)), dma((2,)),
             dma((4,)), dma((4,)),
             dma((3,)), dma((4,)),
             dma((2,)), dma((4,)),
             dma((4,)), dma((4,)),
-            dma((32,)), dma((32,)),
             dma((2, 32)), dma((2, 32)),
+            dma((2, 2, 32)), dma((2, 2, 32)),
             dma((2,)), dma((4,)),
         ],
         compiler_params=pltpu.CompilerParams(
@@ -533,39 +588,39 @@
         at = 8 * b
         inside = (lane >= at) & (lane < at + 8)
         rows = m[b]
-        more = b + 1 < n // 8
-        if more:
-            next_rows = m[b + 1]
-            next_cols = columns_of(next_rows, at)
+        ahead = list(range(b + 1, min(b + 3, n // 8)))
+        ahead_cols = {i: columns_of(m[i], at) for i in ahead}
+        if ahead:
             later = columns_of(rows, at + 8)
-            next_later = columns_of(next_rows, at + 8)
-            next_rows = jnp.where(inside, 0.0, next_rows)
+            next_later = columns_of(m[b + 1], at + 8)
+        ahead_rows = {i: jnp.where(inside, 0.0, m[i]) for i in ahead}
         rows = jnp.where(inside, (lane - at == sub).astype(jnp.float32), rows)
         for j in range(8):
             scale = lax.rsqrt(row_of(cols[j], j))
             below = jnp.where(sub > j, cols[j] * scale, 0.0)
             pivot = row_of(rows, j) * scale
             rows = jnp.where(sub == j, pivot, rows - below * pivot)
-            if more:
-                next_below = next_cols[j] * scale
-                next_rows = next_rows - next_below * pivot
+            ahead_below = {i: ahead_cols[i][j] * scale for i in ahead}
+            for i in ahead:
+                ahead_rows[i] = ahead_rows[i] - ahead_below[i] * pivot
             for k in range(j + 1, 8):
                 row = row_of(cols[k], j) * scale
                 cols[k] = cols[k] - below * row
-                if more:
-                    next_cols[k] = next_cols[k] - next_below * row
-            if more:
+                for i in ahead:
+                    ahead_cols[i][k] = ahead_cols[i][k] - ahead_below[i] * row
+            if ahead:
                 for k in range(8):
                     row = row_of(later[k], j) * scale
                     later[k] = later[k] - below * row
-                    next_later[k] = next_later[k] - next_below * row
+                    next_later[k] = next_later[k] - ahead_below[b + 1] * row
         m[b] = rows
-        if more:
-            m[b + 1] = next_rows
+        for i in ahead:
+            m[i] = ahead_rows[i]
+        if ahead:
             cols = next_later
-        if b + 2 < n // 8:
+        if b + 3 < n // 8:
             change = full_dot(rows, rows, TN)
-            for i in range(b + 2, n // 8):
+            for i in range(b + 3, n // 8):
                 m[i] = jnp.where(inside, 0.0, m[i]) - change[8 * i : 8 * i + 8, :]
     return jnp.concatenate(m, axis=0)
 
@@ -582,10 +637,15 @@
     left_stat_ref[:, 320:] = left_ref[1]
     right_stat_ref[...] = smoothing * right_old_ref[...] + weight * (ours_ref[...] + theirs_ref[...])
     for r in range(4):
+        below, half_row = min(r + 1, 3), r % 2
         for t in range(16):
-            for pair in (0, 1):
-                at = n * r + 8 * t
-                m_ref[at : at + 8, 256 * pair : 256 * pair + 256] = gram_ref[r, 2 * t + pair]
+            at = n * r + 8 * t
+            m_ref[at : at + 8, n * r : n * r + n] = gram_ref[r, t]
+            at = n * below + 8 * t
+            m_ref[at : at + 8, n * (r % 3) : n * (r % 3) + n] = gram_ref[r, 16 + t]
+        for t in range(8):
+            at = n * (2 + half_row) + 64 * (r // 2) + 8 * t
+            m_ref[at : at + 8, n * half_row : n * half_row + n] = gram_ref[r, 32 + t]
         m_ref[order:, n * r : n * r + n] = w_ref[r]
     row = lax.broadcasted_iota(jnp.int32, (n, n), 0)
     col = lax.broadcasted_iota(jnp.int32, (n, n), 1)
@@ -598,8 +658,9 @@
         def _():
             q_ref[...] = panel[order - end :, :]
 
-        if end < order:
-            m_ref[end:, end:] = m_ref[end:, end:] - full_dot(panel, panel[: order - end, :], NT)
+        for to in range(end, order, n):
+            change = full_dot(panel[to - end :, :], panel[to - end : to - end + n, :], NT)
+            m_ref[to:, to : to + n] = m_ref[to:, to : to + n] - change
 
 
 def factor(gram, power, left, squares, ours, theirs, right_old):

time: 88.7 us -> 87 us (0.981)
  Pallas kernels: 85.3 us -> 83.5 us
    pallas_call x1, Pallas kernels: 17.4 us -> 15.5 us  [factor(): pl.pallas_call(factor_kernel, out_shape=(jax.ShapeDtypeStruct((80, 640),...]
where the time goes in v5:
time: 87 us; the launch traced here: 86.8 us
  Pallas kernels  83.5 us (96%)
  local copies, waits for them, and re-layouts  2.59 us (3%)
    pallas_call x1, Pallas kernels, gather_and_power(): pl.pallas_call(main_kernel, out_shape=(jax.ShapeDtypeStruct((4, 40, 8, 12...  68 us
    pallas_call x1, Pallas kernels, factor(): pl.pallas_call(factor_kernel, out_shape=(jax.ShapeDtypeStruct((80, 640),...  15.5 us
    unnamed x8, local copies, waits for them, and re-layouts  2.59 us

profile of v5, /device:TPU:1, one launch (start us, length us, event | category | flops | bytes accessed | tf_op | source)
XLA Modules:
  0.0 86.8 jit_solution(12250845091770257354)
XLA Ops:
  0.6 0.0 copy-start
  0.6 0.0 copy-start.1
  0.7 1.0 %copy-done.1 = f32[80,640]{1,0:T(8,128)S(1)} copy-done((f32[80,640]{1,0:T(8,128)S(1)}, f32[80,640]{1,0:T(8,128)}, u32[]{:S(2)}) %copy-start.1) | copy-done | bytes 204824
  1.6 0.0 copy-start.2
  1.6 0.9 %copy-done.2 = bf16[80,640]{1,0:T(8,128)(2,1)S(1)} copy-done((bf16[80,640]{1,0:T(8,128)(2,1)S(1)}, bf16[80,640]{1,0:T(8,128)(2,1)}, u32[]{:S(2)}) %copy-start.2) | copy-done | bytes 102424
  2.5 0.0 copy-start.3
  2.5 0.7 copy-done.3
  3.2 68.0 %shard_map.67 = (f32[4,40,8,128]{3,2,1,0:T(8,128)S(1)}, f32[4,80,128]{2,1,0:T(8,128)S(1)}, f32[2,80,320]{2,1,0:T(8,128)S(1)}, f32[4,8,128]{2,1,0:T(8,128)S(1)}, ...) custom-call(bf16[80,640]{1,0:T(8,128)(2,1)S(1)} %copy-done.2, bf16[80,128]{1,0:T(8,128)(2,1)S(1)} %copy-done.3, ...), custom_call_target="tpu_custom_call" | custom-call | tf_op jit(solution)/shard_map/pallas_call | solution.py:533
  71.2 0.0 copy-done
  71.3 15.5 %shard_map.68 = (f32[80,640]{1,0:T(8,128)}, f32[80,640]{1,0:T(8,128)}, f32[80,128]{1,0:T(8,128)}) custom-call(f32[4,40,8,128]{3,2,1,0:T(8,128)S(1)} %get-tuple-element.9.gram_ref, f32[4,80,128]{2,1,0:T(8,128)S(1)} %get-tuple-element.10.w_ref, f32[2,80,320]{2,1,0:T(8,128)S(1)} %get-tuple-element.11.left_ref, f32[4,8,128]{2,1,0:T(8,128)S(1)} %get-tuple-element.12.sq_ref, ...), custom_call_target="tpu_custom_call" | custom-call | tf_op jit(solution)/shard_map/pallas_call | solution.py:667
Async XLA Ops:
  0.6 70.6 %copy-start = (f32[80,640]{1,0:T(8,128)S(1)}, f32[80,640]{1,0:T(8,128)}, u32[]{:S(2)}) copy-start(f32[80,640]{1,0:T(8,128)} %right_old_ref.1) | copy-start | bytes 614404
  0.6 1.0 %copy-start.1 = (f32[80,640]{1,0:T(8,128)S(1)}, f32[80,640]{1,0:T(8,128)}, u32[]{:S(2)}) copy-start(f32[80,640]{1,0:T(8,128)} %left_old.1) | copy-start | bytes 614404
  1.6 0.9 %copy-start.2 = (bf16[80,640]{1,0:T(8,128)(2,1)S(1)}, bf16[80,640]{1,0:T(8,128)(2,1)}, u32[]{:S(2)}) copy-start(bf16[80,640]{1,0:T(8,128)(2,1)} %gradient.1) | copy-start | bytes 307204
  2.5 0.7 copy-start.3

commit v6 on v5

--- a/solution.py
+++ b/solution.py
@@ -93,6 +93,18 @@
         at_yh = lax.rem(yh + 1 + lax.rem(turn // 4, 2), 2)
         at_yl = lax.rem(group + at_yh, 2)
         return at_z * 8 + at_yh * 4 + at_x, {"z": at_z, "yh": at_yh, "x": at_x, "yl": at_yl}
+
+    def owner(place):
+        return 5 * place["z"] + place["x"] + place["yh"]
+
+    def owns(place):
+        upper, low = place["yh"] == 1, place["x"] < 2
+        return jnp.logical_or(
+            jnp.logical_and(jnp.logical_not(upper), place["x"] < 3),
+            jnp.logical_and(upper, jnp.logical_not(low)),
+        )
+
+    own_place = {"z": z, "yh": yh, "x": x}
 
     def over_peers(body, init):
         return lax.fori_loop(23, 32, body, lax.fori_loop(0, 22, body, init))
@@ -373,30 +385,29 @@
         block(2 + half_row, half_row),
     )
     for n in (0, 1):
-        for t in range(16):
-            chunk[16 * n + t] = thirds[n][8 * t : 8 * t + 8]
+        for t in range(8):
+            chunk[8 * n + t] = thirds[n][16 * t : 16 * t + 16]
     lower_half = jnp.where(strip_at < 2, thirds[2][:64], thirds[2][64:])
-    for t in range(8):
-        chunk[32 + t] = lower_half[8 * t : 8 * t + 8]
-    doubled = shard < 8
-
-    def scatter_copy(turn, more):
+    for t in range(4):
+        chunk[16 + t] = lower_half[16 * t : 16 * t + 16]
+
+    def scatter_copy(turn):
         other, place = peer(turn)
-        return other, remote(
-            chunk.at[32 * more + other],
-            pieces.at[more, shard],
-            send_rs.at[more, other],
-            recv_rs.at[more, shard],
+        copy = remote(
+            chunk.at[owner(place)],
+            pieces.at[shard],
+            send_rs.at[other],
+            recv_rs.at[shard],
             **place,
         )
+        return place, copy
 
     def scatter_start(turn, _):
-        other, copy = scatter_copy(turn, 0)
-        copy.start()
-
-        @pl.when(other < 8)
+        place, copy = scatter_copy(turn)
+
+        @pl.when(owns(place))
         def _():
-            scatter_copy(turn, 1)[1].start()
+            copy.start()
 
         return 0
 
@@ -419,57 +430,43 @@
 
     def scatter_arrive(turn, total):
         other, _ = peer(turn)
-        arrived(pieces.at[0, other], recv_rs.at[0, other])
-        return total + pieces[0, other]
-
-    def scatter_arrive_more(turn, total):
-        other, _ = peer(turn)
-        arrived(pieces.at[1, other], recv_rs.at[1, other])
-        return total + pieces[1, other]
-
-    def spread_copy(turn, flip, more):
+        arrived(pieces.at[other], recv_rs.at[other])
+        return total + pieces[other]
+
+    def spread_copy(turn, flip):
         other, place = peer(turn)
         if flip:
             place = dict(place, yl=1 - place["yl"])
-        tile = gram.at[strip_at, 32 * more + shard]
-        return remote(
-            tile, tile, send_ag.at[flip, more, other], recv_ag.at[flip, more, shard], **place
-        )
-
-    def spread_all(more):
-        def spread_start(turn, _):
-            spread_copy(turn, 1, more).start()
-            spread_copy(turn, 0, more).start()
-            return 0
-
+        pair = gram.at[strip_at, owner(own_place)]
+        return remote(pair, pair, send_ag.at[flip, other], recv_ag.at[flip, shard], **place)
+
+    def spread_start(turn, _):
+        spread_copy(turn, 1).start()
+        spread_copy(turn, 0).start()
+        return 0
+
+    @pl.when(owns(own_place))
+    def _():
+        gram[strip_at, owner(own_place)] = over_peers(scatter_arrive, chunk[owner(own_place)])
         over_peers(spread_start, 0)
-        spread_copy(22, 1, more).start()
-
-    gram[strip_at, shard] = over_peers(scatter_arrive, chunk[shard])
-    spread_all(0)
-
-    @pl.when(doubled)
-    def _():
-        gram[strip_at, 32 + shard] = over_peers(scatter_arrive_more, chunk[32 + shard])
-        spread_all(1)
+        spread_copy(22, 1).start()
 
     right_product(yl, ours)
 
-    def tile_arrives(flip, other):
+    def pair_arrives(flip, other, place):
         strip = strip_over if flip else strip_at
-        arrived(gram.at[strip, other], recv_ag.at[flip, 0, other])
-
-        @pl.when(other < 8)
+
+        @pl.when(owns(place))
         def _():
-            arrived(gram.at[strip, 32 + other], recv_ag.at[flip, 1, other])
+            arrived(gram.at[strip, owner(place)], recv_ag.at[flip, other])
 
     def spread_arrive(turn, _):
-        other, _ = peer(turn)
-        tile_arrives(1, other)
-        tile_arrives(0, other)
+        other, place = peer(turn)
+        pair_arrives(1, other, place)
+        pair_arrives(0, other, place)
         return 0
 
-    tile_arrives(1, shard)
+    pair_arrives(1, shard, own_place)
     over_peers(spread_arrive, 0)
 
     g_copies = []
@@ -490,28 +487,24 @@
         kept_copy.wait_send()
 
     def drain(turn, _):
-        other, copy = scatter_copy(turn, 0)
-        copy.wait_send()
-        spread_copy(turn, 1, 0).wait_send()
-        spread_copy(turn, 0, 0).wait_send()
-
-        @pl.when(other < 8)
+        place, copy = scatter_copy(turn)
+
+        @pl.when(owns(place))
         def _():
-            scatter_copy(turn, 1)[1].wait_send()
-
-        @pl.when(doubled)
+            copy.wait_send()
+
+        @pl.when(owns(own_place))
         def _():
-            spread_copy(turn, 1, 1).wait_send()
-            spread_copy(turn, 0, 1).wait_send()
+            spread_copy(turn, 1).wait_send()
+            spread_copy(turn, 0).wait_send()
 
         return 0
 
     over_peers(drain, 0)
-    spread_copy(22, 1, 0).wait_send()
-
-    @pl.when(doubled)
+
+    @pl.when(owns(own_place))
     def _():
-        spread_copy(22, 1, 1).wait_send()
+        spread_copy(22, 1).wait_send()
 
     for copy in sq_copies + core_copies + [y_copy, left_copy, right_copy] + w_copies + g_copies:
         copy.wait_send()
@@ -526,14 +519,14 @@
 
 
 def gather_and_power(gradient, basis, left_old):
-    any_space = pl.BlockSpec(memory_space=pl.ANY)
+    any_space = pl.BlockSpec(memory_space=pltpu.HBM)
     vmem = pl.BlockSpec(memory_space=pltpu.VMEM)
     dma = pltpu.SemaphoreType.DMA
     f32, bf16 = jnp.float32, jnp.bfloat16
     return pl.pallas_call(
         main_kernel,
         out_shape=(
-            jax.ShapeDtypeStruct((4, 40, 8, 128), f32),
+            jax.ShapeDtypeStruct((4, 20, 16, 128), f32),
             jax.ShapeDtypeStruct((4, 80, 128), f32),
             jax.ShapeDtypeStruct((2, 80, 320), f32),
             jax.ShapeDtypeStruct((4, 8, 128), f32),
@@ -554,21 +547,21 @@
             pltpu.VMEM((4, 80, 320), f32),
             pltpu.VMEM((2, 80, 128), f32),
             pltpu.VMEM((2, 80, 128), f32),
-            pltpu.VMEM((40, 8, 128), f32),
-            pltpu.VMEM((2, 32, 8, 128), f32),
+            pltpu.VMEM((20, 16, 128), f32),
+            pltpu.VMEM((32, 16, 128), f32),
             dma((2, 3)), dma((2, 2, 16)), dma((64,)), dma((4,)), dma((1,)), dma((4,)), dma((2,)),
             dma((4,)), dma((4,)),
             dma((3,)), dma((4,)),
             dma((2,)), dma((4,)),
             dma((4,)), dma((4,)),
+            dma((32,)), dma((32,)),
             dma((2, 32)), dma((2, 32)),
-            dma((2, 2, 32)), dma((2, 2, 32)),
             dma((2,)), dma((4,)),
         ],
         compiler_params=pltpu.CompilerParams(
             collective_id=0, has_side_effects=True, vmem_limit_bytes=48 << 20
         ),
-    )(gradient, basis, left_old)
+    )(*(pltpu.with_memory_space_constraint(v, pltpu.HBM) for v in (gradient, basis, left_old)))
 
 
 def eliminate(block):
@@ -638,14 +631,14 @@
     right_stat_ref[...] = smoothing * right_old_ref[...] + weight * (ours_ref[...] + theirs_ref[...])
     for r in range(4):
         below, half_row = min(r + 1, 3), r % 2
-        for t in range(16):
-            at = n * r + 8 * t
-            m_ref[at : at + 8, n * r : n * r + n] = gram_ref[r, t]
-            at = n * below + 8 * t
-            m_ref[at : at + 8, n * (r % 3) : n * (r % 3) + n] = gram_ref[r, 16 + t]
         for t in range(8):
-            at = n * (2 + half_row) + 64 * (r // 2) + 8 * t
-            m_ref[at : at + 8, n * half_row : n * half_row + n] = gram_ref[r, 32 + t]
+            at = n * r + 16 * t
+            m_ref[at : at + 16, n * r : n * r + n] = gram_ref[r, t]
+            at = n * below + 16 * t
+            m_ref[at : at + 16, n * (r % 3) : n * (r % 3) + n] = gram_ref[r, 8 + t]
+        for t in range(4):
+            at = n * (2 + half_row) + 64 * (r // 2) + 16 * t
+            m_ref[at : at + 16, n * half_row : n * half_row + n] = gram_ref[r, 16 + t]
         m_ref[order:, n * r : n * r + n] = w_ref[r]
     row = lax.broadcasted_iota(jnp.int32, (n, n), 0)
     col = lax.broadcasted_iota(jnp.int32, (n, n), 1)

time: 87 us -> 84.5 us (0.971)
  local copies, waits for them, and re-layouts: 2.59 us -> 0.01 us
    unnamed x8 -> x2, local copies, waits for them, and re-layouts: 2.59 us -> 0.01 us
where the time goes in v6:
time: 84.5 us; the launch traced here: 84.3 us
  Pallas kernels  83.7 us (99%)
    pallas_call x1, Pallas kernels, gather_and_power(): pl.pallas_call(main_kernel, out_shape=(jax.ShapeDtypeStruct((4, 20, 16, 1...  68.1 us
    pallas_call x1, Pallas kernels, factor(): pl.pallas_call(factor_kernel, out_shape=(jax.ShapeDtypeStruct((80, 640),...  15.5 us

profile of v6, /device:TPU:1, one launch (start us, length us, event | category | flops | bytes accessed | tf_op | source)
XLA Modules:
  0.0 84.3 jit_solution(6587098742314205847)
XLA Ops:
  0.6 0.0 copy-start
  0.6 68.1 %shard_map.67 = (f32[4,20,16,128]{3,2,1,0:T(8,128)S(1)}, f32[4,80,128]{2,1,0:T(8,128)S(1)}, f32[2,80,320]{2,1,0:T(8,128)S(1)}, f32[4,8,128]{2,1,0:T(8,128)S(1)},...) custom-call(bf16[80,640]{1,0:T(8,128)(2,1)} %gradient.1, bf16[80,128]{1,0:T(8,128)(2,1)} %basis.1, f32[80,640]{1,0:T(8,128)} %left_old.1), custom_call_target="tpu_custom_call" | custom-call | tf_op jit(solution)/shard_map/pallas_call | solution.py:526
  68.8 0.0 copy-done
  68.8 15.5 %shard_map.68 = (f32[80,640]{1,0:T(8,128)}, f32[80,640]{1,0:T(8,128)}, f32[80,128]{1,0:T(8,128)}) custom-call(f32[4,20,16,128]{3,2,1,0:T(8,128)S(1)} %get-tuple-element.9.gram_ref, f32[4,80,128]{2,1,0:T(8,128)S(1)} %get-tuple-element.10.w_ref, f32[2,80,320]{2,1,0:T(8,128)S(1)} %get-tuple-element.11.left_ref, f32[4,8,128]{2,1,0:T(8,128)S(1)} %get-tuple-element.12.sq_ref, ...), custom_call_target="tpu_custom_call" | custom-call | tf_op jit(solution)/shard_map/pallas_call | solution.py:660
Async XLA Ops:
  0.6 68.2 %copy-start = (f32[80,640]{1,0:T(8,128)S(1)}, f32[80,640]{1,0:T(8,128)}, u32[]{:S(2)}) copy-start(f32[80,640]{1,0:T(8,128)} %right_old_ref.1) | copy-start | bytes 614404

commit v7 on v6

--- a/solution.py
+++ b/solution.py
@@ -153,8 +153,11 @@
     for h in (0, 1):
         for n, (src, dst) in enumerate(pieces_of(h)):
             copy = give_copy(h, n, src, dst)
-            copy.start()
             waits.append(copy)
+
+            @pl.when(yl != yh)
+            def _():
+                copy.start()
 
             @pl.when(yl == yh)
             def _():
@@ -211,10 +214,16 @@
 
     both = [(k, h, onward) for k, onward in ((yh, 1), (1 - yh, -1)) for h in (0, 1)]
 
-    for k, h, onward in both:
+    for turn, (k, h, onward) in enumerate(both):
         wait_unit(h, k, here[FIRST[h]], here[SECOND[h]])
         step_one(h, k, here[FIRST[h]], here[SECOND[h]], onward)
         step_one(h, k, here[FIRST[h]], here[SECOND[h]], -onward)
+        if turn == 2:
+            @pl.when(yl == yh)
+            def _():
+                for half_at in (0, 1):
+                    for n, (src, dst) in enumerate(pieces_of(half_at)):
+                        give_copy(half_at, n, src, dst).start()
     for toward in (1, -1):
         for k, h, onward in both:
             at_z, at_x = place(h, here[FIRST[h]], here[SECOND[h]])
@@ -331,19 +340,24 @@
     all_squares = jnp.sum(squares[0] + squares[1] + squares[2] + squares[3])
     weight = stat_weight(all_squares)[:1, :1]
 
-    sums = [jnp.zeros((80, 128), jnp.float32)] * 2
+    stacked = []
     for at_z in range(4):
         core_copies[at_z].wait_recv()
         value = stat[at_z] + weight * (partial[at_z] + partial_in[at_z])
         stat[at_z] = value
-        stacked = jnp.concatenate(parts_of(value), axis=0)
-        for k in (0, 1):
-            product = bf16_dot(stacked, blocks[1, k, at_z, :, 256:], NN)
-            sums[k] = sums[k] + (product[:80] + product[80:160] + product[160:])
+        stacked.append(jnp.concatenate(parts_of(value), axis=0))
+    y_copies = []
     for k in (0, 1):
-        power_part[k] = sums[k]
-    y_copy = remote(power_part, power_in, send_one.at[0], recv_one.at[0], yl=1 - yl)
-    y_copy.start()
+        total = jnp.zeros((80, 128), jnp.float32)
+        for at_z in range(4):
+            product = bf16_dot(stacked[at_z], blocks[1, k, at_z, :, 256:], NN)
+            total = total + (product[:80] + product[80:160] + product[160:])
+        power_part[k] = total
+        copy = remote(
+            power_part.at[k], power_in.at[k], send_one.at[4 * k], recv_one.at[4 * k], yl=1 - yl
+        )
+        copy.start()
+        y_copies.append(copy)
     left[yl] = stat[role]
     left_copy = remote(stat.at[across], left.at[yl], send_one.at[1], recv_one.at[1], yl=1 - yl)
     left_copy.start()
@@ -363,9 +377,9 @@
             kept[at_z] = chosen.astype(jnp.bfloat16)
         kept_copy.start()
 
-    y_copy.wait_recv()
     w_copies = []
     for k in (0, 1):
+        y_copies[k].wait_recv()
         slot = 2 * k + core
         power[slot] = power_part[k] + power_in[k]
         copy = remote(power.at[slot], power.at[slot], send_w.at[k], recv_w.at[slot], core=1 - core)
@@ -460,19 +474,20 @@
         def _():
             arrived(gram.at[strip, owner(place)], recv_ag.at[flip, other])
 
-    def spread_arrive(turn, _):
-        other, place = peer(turn)
-        pair_arrives(1, other, place)
-        pair_arrives(0, other, place)
-        return 0
-
-    pair_arrives(1, shard, own_place)
-    over_peers(spread_arrive, 0)
-
     g_copies = []
-    for k in (0, 1):
-        slot = 2 * k + core
-        copy = remote(gram.at[slot], gram.at[slot], send_g.at[k], recv_g.at[slot], core=1 - core)
+    for flip, strip in ((1, strip_over), (0, strip_at)):
+
+        def spread_arrive(turn, _):
+            other, place = peer(turn)
+            pair_arrives(flip, other, place)
+            return 0
+
+        if flip:
+            pair_arrives(1, shard, own_place)
+        over_peers(spread_arrive, 0)
+        copy = remote(
+            gram.at[strip], gram.at[strip], send_g.at[flip], recv_g.at[strip], core=1 - core
+        )
         copy.start()
         g_copies.append(copy)
     for k in (0, 1):
@@ -506,7 +521,7 @@
     def _():
         spread_copy(22, 1).wait_send()
 
-    for copy in sq_copies + core_copies + [y_copy, left_copy, right_copy] + w_copies + g_copies:
+    for copy in sq_copies + core_copies + y_copies + [left_copy, right_copy] + w_copies + g_copies:
         copy.wait_send()
     for copy in waits:
         copy.wait_send()
@@ -553,7 +568,7 @@
             dma((4,)), dma((4,)),
             dma((3,)), dma((4,)),
             dma((2,)), dma((4,)),
-            dma((4,)), dma((4,)),
+            dma((5,)), dma((5,)),
             dma((32,)), dma((32,)),
             dma((2, 32)), dma((2, 32)),
             dma((2,)), dma((4,)),

time: 84.5 us -> 83.5 us (0.988)
  Pallas kernels: 83.7 us -> 82.6 us
    pallas_call x1, Pallas kernels: 68.1 us -> 67.1 us  [gather_and_power(): pl.pallas_call(main_kernel, out_shape=(jax.ShapeDtypeStruct((4, 20, 16, 1...]
where the time goes in v7:
time: 83.5 us; the launch traced here: 83.3 us
  Pallas kernels  82.6 us (99%)
    pallas_call x1, Pallas kernels, gather_and_power(): pl.pallas_call(main_kernel, out_shape=(jax.ShapeDtypeStruct((4, 20, 16, 1...  67.1 us
    pallas_call x1, Pallas kernels, factor(): pl.pallas_call(factor_kernel, out_shape=(jax.ShapeDtypeStruct((80, 640),...  15.5 us

profile of v7, /device:TPU:1, one launch (start us, length us, event | category | flops | bytes accessed | tf_op | source)
XLA Modules:
  0.0 83.3 jit_solution(1422753498415694727)
XLA Ops:
  0.6 0.0 copy-start
  0.6 67.1 %shard_map.67 = (f32[4,20,16,128]{3,2,1,0:T(8,128)S(1)}, f32[4,80,128]{2,1,0:T(8,128)S(1)}, f32[2,80,320]{2,1,0:T(8,128)S(1)}, f32[4,8,128]{2,1,0:T(8,128)S(1)},...) custom-call(bf16[80,640]{1,0:T(8,128)(2,1)} %gradient.1, bf16[80,128]{1,0:T(8,128)(2,1)} %basis.1, f32[80,640]{1,0:T(8,128)} %left_old.1), custom_call_target="tpu_custom_call" | custom-call | tf_op jit(solution)/shard_map/pallas_call | solution.py:541
  67.8 0.0 copy-done
  67.8 15.5 %shard_map.68 = (f32[80,640]{1,0:T(8,128)}, f32[80,640]{1,0:T(8,128)}, f32[80,128]{1,0:T(8,128)}) custom-call(f32[4,20,16,128]{3,2,1,0:T(8,128)S(1)} %get-tuple-element.9.gram_ref, f32[4,80,128]{2,1,0:T(8,128)S(1)} %get-tuple-element.10.w_ref, f32[2,80,320]{2,1,0:T(8,128)S(1)} %get-tuple-element.11.left_ref, f32[4,8,128]{2,1,0:T(8,128)S(1)} %get-tuple-element.12.sq_ref, ...), custom_call_target="tpu_custom_call" | custom-call | tf_op jit(solution)/shard_map/pallas_call | solution.py:675
Async XLA Ops:
  0.6 67.1 %copy-start = (f32[80,640]{1,0:T(8,128)S(1)}, f32[80,640]{1,0:T(8,128)}, u32[]{:S(2)}) copy-start(f32[80,640]{1,0:T(8,128)} %right_old_ref.1) | copy-start | bytes 614404

commit v8 on v7

--- a/solution.py
+++ b/solution.py
@@ -596,7 +596,7 @@
         at = 8 * b
         inside = (lane >= at) & (lane < at + 8)
         rows = m[b]
-        ahead = list(range(b + 1, min(b + 3, n // 8)))
+        ahead = list(range(b + 1, min(b + 4, n // 8)))
         ahead_cols = {i: columns_of(m[i], at) for i in ahead}
         if ahead:
             later = columns_of(rows, at + 8)
@@ -626,9 +626,9 @@
             m[i] = ahead_rows[i]
         if ahead:
             cols = next_later
-        if b + 3 < n // 8:
+        if b + 4 < n // 8:
             change = full_dot(rows, rows, TN)
-            for i in range(b + 3, n // 8):
+            for i in range(b + 4, n // 8):
                 m[i] = jnp.where(inside, 0.0, m[i]) - change[8 * i : 8 * i + 8, :]
     return jnp.concatenate(m, axis=0)
 

time: 83.5 us -> 83.4 us (level)
  no operation moved by 1% of the time
where the time goes in v8:
time: 83.4 us; the launch traced here: 83.2 us
  Pallas kernels  82.5 us (99%)
    pallas_call x1, Pallas kernels, gather_and_power(): pl.pallas_call(main_kernel, out_shape=(jax.ShapeDtypeStruct((4, 20, 16, 1...  67.1 us
    pallas_call x1, Pallas kernels, factor(): pl.pallas_call(factor_kernel, out_shape=(jax.ShapeDtypeStruct((80, 640),...  15.4 us

profile of v8, /device:TPU:1, one launch (start us, length us, event | category | flops | bytes accessed | tf_op | source)
XLA Modules:
  0.0 83.2 jit_solution(3533150178562905580)
XLA Ops:
  0.6 0.0 copy-start
  0.6 67.1 %shard_map.67 = (f32[4,20,16,128]{3,2,1,0:T(8,128)S(1)}, f32[4,80,128]{2,1,0:T(8,128)S(1)}, f32[2,80,320]{2,1,0:T(8,128)S(1)}, f32[4,8,128]{2,1,0:T(8,128)S(1)},...) custom-call(bf16[80,640]{1,0:T(8,128)(2,1)} %gradient.1, bf16[80,128]{1,0:T(8,128)(2,1)} %basis.1, f32[80,640]{1,0:T(8,128)} %left_old.1), custom_call_target="tpu_custom_call" | custom-call | tf_op jit(solution)/shard_map/pallas_call | solution.py:541
  67.8 0.0 copy-done
  67.8 15.4 %shard_map.68 = (f32[80,640]{1,0:T(8,128)}, f32[80,640]{1,0:T(8,128)}, f32[80,128]{1,0:T(8,128)}) custom-call(f32[4,20,16,128]{3,2,1,0:T(8,128)S(1)} %get-tuple-element.9.gram_ref, f32[4,80,128]{2,1,0:T(8,128)S(1)} %get-tuple-element.10.w_ref, f32[2,80,320]{2,1,0:T(8,128)S(1)} %get-tuple-element.11.left_ref, f32[4,8,128]{2,1,0:T(8,128)S(1)} %get-tuple-element.12.sq_ref, ...), custom_call_target="tpu_custom_call" | custom-call | tf_op jit(solution)/shard_map/pallas_call | solution.py:675
Async XLA Ops:
  0.6 67.1 %copy-start = (f32[80,640]{1,0:T(8,128)S(1)}, f32[80,640]{1,0:T(8,128)}, u32[]{:S(2)}) copy-start(f32[80,640]{1,0:T(8,128)} %right_old_ref.1) | copy-start | bytes 614404
